TPU v7x, 512 devices: a whole 4x4x16 slice. The times are simulated.
512 devices in a mesh: dom: 16 (over x, y_lo, core), shard: 32 (over y_hi, z).
Axes of the slice: x: 4, y: 4 (y_hi: 2, y_lo: 2; y = y_hi * 2 + y_lo), z: 16, core: 2. Of those that a mesh axis runs over, the one named last changes fastest.
Arguments:
- embeddings: float32 [32768, 400], P(('dom', 'shard')), may hold values from -3 to 3
- row_accum: float32 [32768], P(('dom', 'shard')), may hold values from 0.01 to 1
- relations: bfloat16 [2560, 400], replicated, may hold values from -3 to 3
- relation_accum: float32 [2560], P(('dom', 'shard')), may hold values from 0.01 to 1
- request_rows: int32 [2, 16384, 2, 16], P(None, ('dom', 'shard')), may hold values from 0 to 63
- head_slots: int32 [2, 65536], P(None, ('dom', 'shard')), may hold values from 0 to 511
- tail_slots: int32 [2, 65536], P(None, ('dom', 'shard')), may hold values from 0 to 511
- relation_ids: int32 [2, 65536], P(None, ('dom', 'shard')), may hold values from 0 to 2559
- own_negatives: int32 [2, 262144], P(None, ('dom', 'shard')), may hold values from 0 to 511
- far_negatives: int32 [2, 262144], P(None, ('dom', 'shard')), may hold values from 0 to 511
Outputs:
- new_embeddings: float32 [32768, 400], P(('dom', 'shard'))
- new_accum: float32 [32768], P(('dom', 'shard'))
- relation_step: float32 [2560, 400], P(('dom', 'shard'))
- new_relation_accum: float32 [2560], P(('dom', 'shard'))
Inputs may be any that keep to these rules, and one draw needn't show every extreme that they name: `request_rows`: local row numbers within the owner's 64 rows. `head_slots`: slots of the 512 own-side touched rows. `tail_slots`: slots of the 512 partner-side touched rows. `own_negatives`: slots of the 512 own-side touched rows. `far_negatives`: slots of the 512 partner-side touched rows.
All inputs are finite; a program needn't handle non-finite values.
Results may differ from a plain program's by a relative error of at most 0.0049.
Values may be sent and summed in bfloat16 or wider, within the bound.
A program may use at most 64 MiB of HBM per device.

v0:
```python
import jax
import jax.numpy as jnp
from jax import lax
from jax.sharding import PartitionSpec as P

LEARN_RATE = 0.1


def partner(value, axis, distance):
    mask = 2**distance
    pairs = [(source, source ^ mask) for source in range(lax.axis_size(axis))]
    return lax.ppermute(value, axis, pairs)


def edge_terms(
    own_touched,
    far_touched,
    head_slots,
    tail_slots,
    relation_ids,
    own_negatives,
    far_negatives,
    relations,
):
    neg_count = own_negatives.shape[0]
    head_vec = own_touched[head_slots].astype(jnp.float32)
    tail_vec = far_touched[tail_slots].astype(jnp.float32)
    rel_vec = relations[relation_ids].astype(jnp.float32)
    positive = jnp.sum(head_vec * rel_vec * tail_vec, axis=-1)
    query_tail = (head_vec * rel_vec).astype(jnp.bfloat16)
    query_head = (tail_vec * rel_vec).astype(jnp.bfloat16)
    neg_tail = far_touched[far_negatives]
    neg_head = own_touched[own_negatives]
    contract_last = (((1,), (1,)), ((), ()))
    contract_first = (((0,), (0,)), ((), ()))
    score_tail = lax.dot_general(
        query_tail, neg_tail, contract_last, preferred_element_type=jnp.float32
    )
    score_head = lax.dot_general(
        query_head, neg_head, contract_last, preferred_element_type=jnp.float32
    )
    weight_tail = (jax.nn.sigmoid(score_tail) / neg_count).astype(jnp.bfloat16)
    weight_head = (jax.nn.sigmoid(score_head) / neg_count).astype(jnp.bfloat16)
    back_tail = jnp.dot(weight_tail, neg_tail, preferred_element_type=jnp.float32)
    back_head = jnp.dot(weight_head, neg_head, preferred_element_type=jnp.float32)
    coeff = -jax.nn.sigmoid(-positive)[:, None]
    grad_head = coeff * rel_vec * tail_vec + rel_vec * back_tail
    grad_tail = coeff * head_vec * rel_vec + rel_vec * back_head
    grad_rel = coeff * head_vec * tail_vec + head_vec * back_tail + tail_vec * back_head
    grad_negtail = lax.dot_general(
        weight_tail, query_tail, contract_first, preferred_element_type=jnp.float32
    )
    grad_neghead = lax.dot_general(
        weight_head, query_head, contract_first, preferred_element_type=jnp.float32
    )
    touch_rows = own_touched.shape[0]
    emb_width = own_touched.shape[1]
    own_grad = (
        jnp.zeros((touch_rows, emb_width), jnp.float32)
        .at[head_slots]
        .add(grad_head)
        .at[own_negatives]
        .add(grad_neghead)
    )
    far_grad = (
        jnp.zeros((touch_rows, emb_width), jnp.float32)
        .at[tail_slots]
        .add(grad_tail)
        .at[far_negatives]
        .add(grad_negtail)
    )
    return (own_grad.astype(jnp.bfloat16), far_grad.astype(jnp.bfloat16), grad_rel)


def body(
    embeddings,
    row_accum,
    relations,
    relation_accum,
    request_rows,
    head_slots,
    tail_slots,
    relation_ids,
    own_negatives,
    far_negatives,
):
    row_count, emb_width = embeddings.shape
    shard_count = lax.axis_size("shard")
    slot_count = request_rows.shape[-1]
    touch_rows = shard_count * slot_count
    emb_table = embeddings
    accum_now = row_accum
    relation_grad = jnp.zeros((relations.shape[0], emb_width), jnp.float32)
    for r in range(request_rows.shape[0]):
        lowered = emb_table.astype(jnp.bfloat16)
        request_ids = request_rows[r]
        served = lowered[request_ids]
        received = lax.all_to_all(served, "shard", split_axis=0, concat_axis=0, tiled=True)
        own_touched = received[:, 0].reshape(touch_rows, emb_width)
        far_touched = partner(received[:, 1].reshape(touch_rows, emb_width), "dom", r)
        own_grad, far_grad, grad_rel = edge_terms(
            own_touched,
            far_touched,
            head_slots[r],
            tail_slots[r],
            relation_ids[r],
            own_negatives[r],
            far_negatives[r],
            relations,
        )
        relation_grad = relation_grad.at[relation_ids[r]].add(grad_rel)
        far_back = partner(far_grad, "dom", r)
        outgoing = jnp.stack(
            [
                own_grad.reshape(shard_count, slot_count, emb_width),
                far_back.reshape(shard_count, slot_count, emb_width),
            ],
            axis=1,
        )
        returned = lax.all_to_all(outgoing, "shard", split_axis=0, concat_axis=0, tiled=True)
        row_grad = (
            jnp.zeros((row_count, emb_width), jnp.float32)
            .at[request_ids.reshape(-1)]
            .add(returned.reshape(-1, emb_width).astype(jnp.float32))
        )
        accum_now = accum_now + jnp.mean(row_grad * row_grad, axis=-1)
        emb_table = emb_table - LEARN_RATE * row_grad / jnp.sqrt(accum_now)[:, None]
    own_share = lax.psum_scatter(relation_grad, ("dom", "shard"), scatter_dimension=0, tiled=True)
    new_relation_accum = relation_accum + jnp.mean(own_share * own_share, axis=-1)
    relation_step = -LEARN_RATE * own_share / jnp.sqrt(new_relation_accum)[:, None]
    return (emb_table, accum_now, relation_step, new_relation_accum)


def solution(mesh):
    placed = (
        P(("dom", "shard"), None),
        P(("dom", "shard")),
        P(),
        P(("dom", "shard")),
        P(None, ("dom", "shard"), None, None),
        P(None, ("dom", "shard")),
        P(None, ("dom", "shard")),
        P(None, ("dom", "shard")),
        P(None, ("dom", "shard")),
        P(None, ("dom", "shard")),
    )
    return jax.shard_map(
        body,
        mesh=mesh,
        in_specs=placed,
        out_specs=(
            P(("dom", "shard"), None),
            P(("dom", "shard")),
            P(("dom", "shard"), None),
            P(("dom", "shard")),
        ),
        check_vma=False,
    )
```

profile of v0, /device:TPU:6, one launch (start us, length us, event | category | flops | bytes accessed | tf_op | source)
XLA Modules:
  0.0 834.3 jit_solution(16513488872124528035)
XLA Ops:
  7.2 0.9 convert_element_type.72
  8.1 0.7 compare_select_fusion
  9.0 5.0 gather_fusion
  14.1 18.2 %all-to-all-start = ((bf16[32,2,16,400]{3,2,1,0:T(8,128)(2,1)}), bf16[32,2,16,400]{3,2,1,0:T(8,128)(2,1)}, u32[]{:S(2)}, u32[]{:S(2)}) async-start(bf16[32,2,16,400]{3,2,1,0:T(8,128)(2,1)} %bitcast.4), calls=%async_computation | async-start | bytes 2097152 | tf_op jit(solution)/shard_map/all_to_all | solution.py:98
  32.4 2.9 copy.50
  35.3 0.8 gather_fusion.2
  36.4 0.4 copy-done
  36.8 48.0 %all-to-all-done = bf16[32,2,16,400]{3,2,1,0:T(8,128)(2,1)} async-done(((bf16[32,2,16,400]{3,2,1,0:T(8,128)(2,1)}), bf16[32,2,16,400]{3,2,1,0:T(8,128)(2,1)}, u32[]{:S(2)}, u32[]{:S(2)}) %all-to-all-start) | async-done | bytes 819232 | tf_op jit(solution)/shard_map/all_to_all | solution.py:98
  84.7 1.3 fusion.73
  86.0 1.9 collective-permute-start
  88.0 0.8 gather_fusion.1
  88.9 2.0 gather_fusion.5
  90.9 0.8 gather_fusion.3
  91.9 0.4 fusion.23
  92.3 0.3 fusion.75
  92.7 2.0 gather_fusion.4
  94.7 0.4 fusion.22
  95.0 0.3 fusion.53
  95.4 0.3 fusion.37
  95.9 1.6 scatter_custom_fusion.2
  97.4 4.0 scatter_fusion.1
  101.5 2.4 collective-permute-start.1
  104.1 1.6 scatter_custom_fusion
  105.7 0.3 fusion.59
  106.0 4.2 scatter_fusion
  110.3 2.2 pad_maximum_fusion
  112.5 7.9 all-to-all-start.1
  120.9 52.1 %all-to-all-done.1 = bf16[32,2,16,400]{3,2,1,0:T(8,128)(2,1)S(1)} async-done(((bf16[32,2,16,400]{3,2,1,0:T(8,128)(2,1)}), bf16[32,2,16,400]{3,2,1,0:T(8,128)(2,1)S(1)}, u32[]{:S(2)}, u32[]{:S(2)}) %all-to-all-start.1) | async-done | bytes 819232 | tf_op jit(solution)/shard_map/all_to_all | solution.py:120
  172.9 6.8 scatter_custom_fusion.4
  179.9 4.0 gather_fusion.6
  183.9 60.2 %all_to_all.20 = bf16[32,2,16,400]{3,2,1,0:T(8,128)(2,1)S(1)} all-to-all(bf16[32,2,16,400]{3,2,1,0:T(8,128)(2,1)S(1)} %bitcast.88), channel_id=1, replica_groups=mesh['dom'=16,'shard'=32] {'shard'}, dimensions={0} | all-to-all | bytes 1638400 | tf_op jit(solution)/shard_map/all_to_all | solution.py:98
  244.2 2.6 collective-permute-start.2
  246.8 3.0 gather_fusion.8
  249.9 0.8 gather_fusion.7
  250.9 2.0 gather_fusion.11
  252.9 5.4 collective-permute-done.2
  258.3 0.8 gather_fusion.9
  259.3 0.4 fusion.25
  259.6 0.3 fusion.76
  260.1 2.0 gather_fusion.10
  262.0 0.4 fusion.24
  262.4 0.3 fusion.50
  262.7 0.3 fusion.39
  263.1 0.8 copy.67
  263.9 2.0 scatter_custom_fusion.7
  265.9 4.2 scatter_fusion.3
  270.1 0.9 convert_element_type.93
  271.0 2.6 collective-permute-start.3
  273.6 0.1 copy.65
  273.7 1.6 scatter_custom_fusion.5
  275.3 0.3 fusion.56
  275.7 4.0 scatter_fusion.2
  279.7 4.8 collective-permute-done.3
  284.5 2.1 pad_maximum_fusion.1
  286.7 11.1 %all-to-all-start.3 = ((bf16[32,2,16,400]{3,2,1,0:T(8,128)(2,1)}), bf16[32,2,16,400]{3,2,1,0:T(8,128)(2,1)S(1)}, u32[]{:S(2)}, u32[]{:S(2)}) async-start(bf16[32,2,16,400]{3,2,1,0:T(8,128)(2,1)} %pad_maximum_fusion.1), calls=%async_computation.3 | async-start | bytes 2097152 | tf_op jit(solution)/shard_map/all_to_all | solution.py:120
  297.9 4.0 scatter_custom_fusion.10
  302.0 6.1 scatter_fusion.4
  308.4 508.1 %all-reduce.3.cloned.1.call-done = f32[2560,400]{1,0:T(8,128)} async-done(((f32[2560,400]{1,0:T(8,128)}), f32[2560,400]{1,0:T(8,128)}) %all-reduce.3.cloned.1.call-update) | async-done | bytes 4096016
  816.5 0.9 multiply_reduce_fusion.2
  817.4 0.5 fusion.70
  817.9 1.4 multiply_divide_fusion
  819.3 6.8 scatter_custom_fusion.9
  826.2 0.5 fusion.71
  826.7 0.8 divide_subtract_fusion
  (72 shorter events, 3.0 us)
Async XLA Ops:
  14.1 70.7 %all-to-all-start = ((bf16[32,2,16,400]{3,2,1,0:T(8,128)(2,1)}), bf16[32,2,16,400]{3,2,1,0:T(8,128)(2,1)}, u32[]{:S(2)}, u32[]{:S(2)}) async-start(bf16[32,2,16,400]{3,2,1,0:T(8,128)(2,1)} %bitcast.4), calls=%async_computation | async-start | bytes 2097152 | tf_op jit(solution)/shard_map/all_to_all | solution.py:98
  32.3 2.9 copy-start.5
  32.3 4.0 copy-start.6
  32.3 4.0 copy-start.3
  32.3 4.0 copy-start.4
  35.3 1.5 copy-start
  35.3 52.7 %copy-start.7 = (s32[2,128]{1,0:T(2,128)S(1)}, s32[2,128]{1,0:T(2,128)}, u32[]{:S(2)}) copy-start(s32[2,128]{1,0:T(2,128)} %param.15) | copy-start | bytes 3076
  86.0 4.9 collective-permute-start
  101.5 8.7 %collective-permute-start.1 = (bf16[512,400]{1,0:T(8,128)(2,1)S(1)}, bf16[512,400]{1,0:T(8,128)(2,1)}, u32[]{:S(2)}, u32[]{:S(2)}) collective-permute-start(bf16[512,400]{1,0:T(8,128)(2,1)S(1)} %convert_element_type.81), channel_id=1, source_target_pairs={{0,32},{32,0},{64,96},{96,64},{128,160},{160,128},{192,224},{224,1... | collective-permute-start | bytes 1228808 | tf_op jit(solution)/shard_map/ppermute | solution.py:12
  110.2 10.3 %copy-start.2 = (s32[2,32,2,16]{1,3,2,0:T(8,128)S(1)}, s32[2,32,2,16]{1,3,2,0:T(8,128)}, u32[]{:S(2)}) copy-start(s32[2,32,2,16]{1,3,2,0:T(8,128)} %param.14) | copy-start | bytes 24580
  110.3 69.5 %copy-start.8 = (f32[64]{0:T(128)S(1)}, f32[64]{0:T(128)}, u32[]{:S(2)}) copy-start(f32[64]{0:T(128)} %param.11) | copy-start | bytes 772
  110.3 69.6 %copy-start.1 = (f32[64,400]{1,0:T(8,128)S(1)}, f32[64,400]{1,0:T(8,128)}, u32[]{:S(2)}) copy-start(f32[64,400]{1,0:T(8,128)} %param.10) | copy-start | bytes 307204
  112.5 60.5 %all-to-all-start.1 = ((bf16[32,2,16,400]{3,2,1,0:T(8,128)(2,1)}), bf16[32,2,16,400]{3,2,1,0:T(8,128)(2,1)S(1)}, u32[]{:S(2)}, u32[]{:S(2)}) async-start(bf16[32,2,16,400]{3,2,1,0:T(8,128)(2,1)} %pad_maximum_fusion), calls=%async_computation.1 | async-start | bytes 2097152 | tf_op jit(solution)/shard_map/all_to_all | solution.py:120
  244.2 14.1 %collective-permute-start.2 = (bf16[512,400]{1,0:T(8,128)(2,1)S(1)}, bf16[512,400]{1,0:T(8,128)(2,1)S(1)}, u32[]{:S(2)}, u32[]{:S(2)}) collective-permute-start(bf16[512,400]{1,0:T(8,128)(2,1)S(1)} %bitcast.93), channel_id=1, source_target_pairs={{0,64},{32,96},{64,0},{96,32},{128,192},{160,224},{192,128},{224,1... | collective-permute-start | bytes 1228808 | tf_op jit(solution)/shard_map/ppermute | solution.py:12
  271.0 13.5 %collective-permute-start.3 = (bf16[512,400]{1,0:T(8,128)(2,1)}, bf16[512,400]{1,0:T(8,128)(2,1)}, u32[]{:S(2)}, u32[]{:S(2)}) collective-permute-start(bf16[512,400]{1,0:T(8,128)(2,1)} %convert_element_type.93), channel_id=1, source_target_pairs={{0,64},{32,96},{64,0},{96,32},{128,192},{160,224},{192,128},{224,1... | collective-permute-start | bytes 1228808 | tf_op jit(solution)/shard_map/ppermute | solution.py:12
  286.7 532.7 %all-to-all-start.3 = ((bf16[32,2,16,400]{3,2,1,0:T(8,128)(2,1)}), bf16[32,2,16,400]{3,2,1,0:T(8,128)(2,1)S(1)}, u32[]{:S(2)}, u32[]{:S(2)}) async-start(bf16[32,2,16,400]{3,2,1,0:T(8,128)(2,1)} %pad_maximum_fusion.1), calls=%async_computation.3 | async-start | bytes 2097152 | tf_op jit(solution)/shard_map/all_to_all | solution.py:120
  297.7 518.8 %all-reduce.3.cloned.1.call-start = ((), (), s32[]{:S(2)}) async-start(), calls=%async_computation.4 | async-start | bytes 10485760
  308.1 509.2 %copy-start.9 = (f32[5]{0:T(128)S(1)}, f32[5]{0:T(128)}, u32[]{:S(2)}) copy-start(f32[5]{0:T(128)} %param.13) | copy-start | bytes 64
Sparse Core Ops, SparseCore 0:
  308.3 508.1 all-reduce.2
where the time goes:
time: 835 us; the launch traced here: 834 us
  waiting for transfers between devices  618 us (74%)
  blocking collectives  60.2 us (7%)
  other arithmetic  58.5 us (7%)
  starting transfers between devices  46.8 us (6%)
  local copies, waits for them, and re-layouts  31.7 us (4%)
  between operations  14.7 us (2%)
    unnamed x2, waiting for transfers between devices  508 us
    all_to_all x1, blocking collectives, body(): lax.all_to_all(served, 'shard', split_axis=0, concat_axis=0, tiled=True)  60.2 us
    all_to_all x2, waiting for transfers between devices, body(): lax.all_to_all(outgoing, 'shard', split_axis=0, concat_axis=0, tiled=True)  52.1 us
    all_to_all x1, waiting for transfers between devices, body(): lax.all_to_all(served, 'shard', split_axis=0, concat_axis=0, tiled=True)  48 us
    all_to_all x2, starting transfers between devices, body(): lax.all_to_all(outgoing, 'shard', split_axis=0, concat_axis=0, tiled=True)  19 us
    all_to_all x1, starting transfers between devices, body(): lax.all_to_all(served, 'shard', split_axis=0, concat_axis=0, tiled=True)  18.2 us
  transfers between devices with their start and end apart: 8, of which 5 were waited for; matrix products, arithmetic and copies ran while one was open for 5% of the time, Pallas kernels for 0%

commit v1 on v0

v1 whole, which is shorter than its diff:
```python
import jax
import jax.numpy as jnp
from jax import lax
from jax.sharding import PartitionSpec as P

LEARN_RATE = 0.1
BF = jnp.bfloat16
F32 = jnp.float32


def partner(value, axis, distance):
    mask = 2**distance
    pairs = [(source, source ^ mask) for source in range(lax.axis_size(axis))]
    return lax.ppermute(value, axis, pairs)


def mm(a, b, ca, cb):
    return lax.dot_general(a, b, (((ca,), (cb,)), ((), ())), preferred_element_type=F32)


def one_hot(ids, n):
    return (ids[:, None] == jnp.arange(n, dtype=ids.dtype)[None, :]).astype(BF)


def split_mm(a, b, ca, cb):
    hi = b.astype(BF)
    lo = (b - hi.astype(F32)).astype(BF)
    return mm(a, hi, ca, cb) + mm(a, lo, ca, cb)


def edge_terms(own, far, head_slots, tail_slots, rel_vec, own_neg, far_neg):
    touch = own.shape[0]
    neg = own_neg.shape[0]
    head_hot = one_hot(head_slots, touch)
    tail_hot = one_hot(tail_slots, touch)
    head_vec = mm(head_hot, own, 1, 0)
    tail_vec = mm(tail_hot, far, 1, 0)
    slots = jnp.arange(touch, dtype=own_neg.dtype)
    own_count = jnp.sum((own_neg[:, None] == slots[None, :]).astype(F32), axis=0)
    far_count = jnp.sum((far_neg[:, None] == slots[None, :]).astype(F32), axis=0)
    positive = jnp.sum(head_vec * rel_vec * tail_vec, axis=-1)
    query_tail = (head_vec * rel_vec).astype(BF)
    query_head = (tail_vec * rel_vec).astype(BF)
    score_tail = mm(query_tail, far, 1, 1)
    score_head = mm(query_head, own, 1, 1)
    weight_tail = (jax.nn.sigmoid(score_tail) * (far_count / neg)).astype(BF)
    weight_head = (jax.nn.sigmoid(score_head) * (own_count / neg)).astype(BF)
    back_tail = mm(weight_tail, far, 1, 0)
    back_head = mm(weight_head, own, 1, 0)
    coeff = -jax.nn.sigmoid(-positive)[:, None]
    grad_head = rel_vec * (coeff * tail_vec + back_tail)
    grad_tail = rel_vec * (coeff * head_vec + back_head)
    grad_rel = coeff * head_vec * tail_vec + head_vec * back_tail + tail_vec * back_head
    own_grad = split_mm(head_hot, grad_head, 0, 0) + mm(weight_head, query_head, 0, 0)
    far_grad = split_mm(tail_hot, grad_tail, 0, 0) + mm(weight_tail, query_tail, 0, 0)
    return own_grad.astype(BF), far_grad.astype(BF), grad_rel


def body(embeddings, row_accum, relations, relation_accum, request_rows, head_slots, tail_slots, relation_ids, own_negatives, far_negatives):
    rows, width = embeddings.shape
    shards = lax.axis_size("shard")
    slot_count = request_rows.shape[-1]
    touch = shards * slot_count
    rounds = request_rows.shape[0]
    emb = embeddings
    accum = row_accum
    rel_rows = []
    all_rel = relations[relation_ids.reshape(-1)].astype(F32).reshape(rounds, -1, width)
    for r in range(rounds):
        lowered = emb.astype(BF)
        ids = request_rows[r].reshape(-1)
        hot = one_hot(ids, rows)
        served = mm(hot, lowered, 1, 0).astype(BF).reshape(shards, 2, slot_count, width)
        received = lax.all_to_all(served, "shard", split_axis=0, concat_axis=0, tiled=True)
        own = received[:, 0].reshape(touch, width)
        far = partner(received[:, 1].reshape(touch, width), "dom", r)
        own_grad, far_grad, grad_rel = edge_terms(
            own, far, head_slots[r], tail_slots[r], all_rel[r], own_negatives[r], far_negatives[r]
        )
        rel_rows.append(grad_rel.astype(BF))
        far_back = partner(far_grad, "dom", r)
        outgoing = jnp.stack(
            [own_grad.reshape(shards, slot_count, width), far_back.reshape(shards, slot_count, width)], axis=1
        )
        returned = lax.all_to_all(outgoing, "shard", split_axis=0, concat_axis=0, tiled=True)
        row_grad = mm(hot, returned.reshape(-1, width), 0, 0)
        accum = accum + jnp.mean(row_grad * row_grad, axis=-1)
        emb = emb - LEARN_RATE * row_grad / jnp.sqrt(accum)[:, None]
    mine = jnp.concatenate(rel_rows, axis=0)
    ids = lax.all_gather(relation_ids.reshape(-1), "dom", tiled=True)
    group_rows = lax.all_gather(mine, "dom", tiled=True)
    per_group = relations.shape[0] // lax.axis_size("dom")
    local = ids - lax.axis_index("dom").astype(ids.dtype) * per_group
    dense = mm(one_hot(local, per_group), group_rows, 0, 0)
    pieces = dense.reshape(shards, per_group // shards, width)
    pieces = lax.all_to_all(pieces, "shard", split_axis=0, concat_axis=0, tiled=True)
    own_share = jnp.sum(pieces, axis=0)
    new_relation_accum = relation_accum + jnp.mean(own_share * own_share, axis=-1)
    relation_step = -LEARN_RATE * own_share / jnp.sqrt(new_relation_accum)[:, None]
    return (emb, accum, relation_step, new_relation_accum)


def solution(mesh):
    both = ("dom", "shard")
    return jax.shard_map(
        body,
        mesh=mesh,
        in_specs=(P(both, None), P(both), P(), P(both), P(None, both, None, None)) + (P(None, both),) * 5,
        out_specs=(P(both, None), P(both), P(both, None), P(both)),
        check_vma=False,
    )
```

time: 835 us -> 353 us (0.42)
  waiting for transfers between devices: 618 us -> 225 us
  other arithmetic: 58.5 us -> 5.68 us
  blocking collectives: 60.2 us -> 15.7 us
  local copies, waits for them, and re-layouts: 31.7 us -> 14.4 us
  starting transfers between devices: 46.8 us -> 62.1 us
  matrix products: 4.09 us -> 14.3 us
    unnamed x2 -> x1, waiting for transfers between devices: 508 us -> 0.02 us
    all_to_all x1 -> x0, blocking collectives: 60.2 us -> none  [body(): lax.all_to_all(served, 'shard', split_axis=0, concat_axis=0, tiled=True)]
    all_to_all x1 -> x2, waiting for transfers between devices: 48 us -> 99.6 us  [body(): lax.all_to_all(served, 'shard', split_axis=0, concat_axis=0, tiled=True)]
    scatter-add x12 -> x0, other arithmetic: 46.7 us -> none  [the longest x2 13.5 us: body(): row_grad = jnp.zeros((row_count, emb_width), jnp.float32).at[request_ids....]
    all_to_all x2, waiting for transfers between devices: 52.1 us -> 78.6 us  [body(): lax.all_to_all(outgoing, 'shard', split_axis=0, concat_axis=0, tiled=True)]
    gather x18 -> x2, local copies, waits for them, and re-layouts: 24.8 us -> 1.29 us  [body(): relations[relation_ids.reshape(-1)].astype(F32).reshape(rounds, -1, width)]
    all_to_all x0 -> x1, waiting for transfers between devices: none -> 21.2 us  [body(): lax.all_to_all(pieces, 'shard', split_axis=0, concat_axis=0, tiled=True)]
    all_gather x0 -> x1, blocking collectives: none -> 15.7 us  [body(): ids = lax.all_gather(relation_ids.reshape(-1), 'dom', tiled=True)]
  transfers between devices with their start and end apart: 8 -> 10, of which waited for: 5 -> 10; matrix products, arithmetic and copies ran while one was open for 5% -> 5% of each run, Pallas kernels for 0% -> 0%
where the time goes in v1:
time: 353 us; the launch traced here: 352 us
  waiting for transfers between devices  225 us (64%)
  starting transfers between devices  62.1 us (18%)
  blocking collectives  15.7 us (4%)
  between operations  14.6 us (4%)
  local copies, waits for them, and re-layouts  14.4 us (4%)
  matrix products  14.3 us (4%)
  other arithmetic  5.68 us (2%)
    all_to_all x2, waiting for transfers between devices, body(): lax.all_to_all(served, 'shard', split_axis=0, concat_axis=0, tiled=True)  99.6 us
    all_to_all x2, waiting for transfers between devices, body(): lax.all_to_all(outgoing, 'shard', split_axis=0, concat_axis=0, tiled=True)  78.6 us
    all_to_all x2, starting transfers between devices, body(): lax.all_to_all(served, 'shard', split_axis=0, concat_axis=0, tiled=True)  26.4 us
    all_to_all x1, waiting for transfers between devices, body(): lax.all_to_all(pieces, 'shard', split_axis=0, concat_axis=0, tiled=True)  21.2 us
    ppermute x4, waiting for transfers between devices, partner(): return lax.ppermute(value, axis, pairs)  20.5 us
    all_to_all x2, starting transfers between devices, body(): lax.all_to_all(outgoing, 'shard', split_axis=0, concat_axis=0, tiled=True)  18.9 us
    all_gather x1, blocking collectives, body(): ids = lax.all_gather(relation_ids.reshape(-1), 'dom', tiled=True)  15.7 us
    dot_general x29, matrix products, mm(): lax.dot_general(a, b, (((ca,), (cb,)), ((), ())), preferred_element_type=...  14.3 us
  transfers between devices with their start and end apart: 10, of which 10 were waited for; matrix products, arithmetic and copies ran while one was open for 5% of the time, Pallas kernels for 0%

profile of v1, /device:TPU:6, one launch (start us, length us, event | category | flops | bytes accessed | tf_op | source)
XLA Modules:
  0.0 351.7 jit_solution(11925494591055917611)
XLA Ops:
  7.2 0.7 fusion.69
  8.1 1.5 convolution_convert_fusion.1
  9.6 1.3 copy.43
  10.9 18.2 %all-to-all-start = ((bf16[32,2,16,400]{3,2,1,0:T(8,128)(2,1)}), bf16[32,2,16,400]{3,2,1,0:T(8,128)(2,1)}, u32[]{:S(2)}, u32[]{:S(2)}) async-start(bf16[32,2,16,400]{3,2,1,0:T(8,128)(2,1)} %bitcast.3), calls=%async_computation | async-start | bytes 2097152 | tf_op jit(solution)/shard_map/all_to_all | solution.py:74
  29.1 2.9 copy.41
  32.1 1.2 gather_fusion
  33.9 47.7 %all-to-all-done = bf16[32,2,16,400]{3,2,1,0:T(8,128)(2,1)} async-done(((bf16[32,2,16,400]{3,2,1,0:T(8,128)(2,1)}), bf16[32,2,16,400]{3,2,1,0:T(8,128)(2,1)}, u32[]{:S(2)}, u32[]{:S(2)}) %all-to-all-start) | async-done | bytes 819232 | tf_op jit(solution)/shard_map/all_to_all | solution.py:74
  81.5 1.3 fusion.68
  82.8 1.9 collective-permute-start
  84.8 1.8 collective-permute-done
  86.6 0.4 fusion.35
  87.0 0.4 fusion.52
  87.4 0.4 fusion.22
  87.8 0.3 add_multiply_fusion.3
  88.1 0.4 fusion.23
  88.5 0.3 add_convert_fusion.1
  88.8 0.4 fusion.34
  89.2 0.4 convolution_add_fusion.6
  89.5 0.2 fusion.3
  89.8 2.0 collective-permute-start.1
  91.8 0.3 fusion.36
  92.2 0.3 convolution_add_fusion.7
  93.0 0.4 collective-permute-done.1
  93.8 1.1 copy.46
  94.8 7.9 %all-to-all-start.1 = ((bf16[32,2,16,400]{3,2,1,0:T(8,128)(2,1)}), bf16[32,2,16,400]{3,2,1,0:T(8,128)(2,1)S(1)}, u32[]{:S(2)}, u32[]{:S(2)}) async-start(bf16[32,2,16,400]{3,2,1,0:T(8,128)(2,1)} %copy.46), calls=%async_computation.1 | async-start | bytes 2097152 | tf_op jit(solution)/shard_map/all_to_all | solution.py:85
  103.0 52.4 %all-to-all-done.1 = bf16[32,2,16,400]{3,2,1,0:T(8,128)(2,1)S(1)} async-done(((bf16[32,2,16,400]{3,2,1,0:T(8,128)(2,1)}), bf16[32,2,16,400]{3,2,1,0:T(8,128)(2,1)S(1)}, u32[]{:S(2)}, u32[]{:S(2)}) %all-to-all-start.1) | async-done | bytes 819232 | tf_op jit(solution)/shard_map/all_to_all | solution.py:85
  155.3 0.6 multiply_reduce_fusion.3
  155.9 0.6 convolution_convert_fusion
  156.5 1.3 copy.48
  157.8 8.1 %all-to-all-start.2 = ((bf16[32,2,16,400]{3,2,1,0:T(8,128)(2,1)}), bf16[32,2,16,400]{3,2,1,0:T(8,128)(2,1)S(1)}, u32[]{:S(2)}, u32[]{:S(2)}) async-start(bf16[32,2,16,400]{3,2,1,0:T(8,128)(2,1)} %bitcast.13), calls=%async_computation.2 | async-start | bytes 2097152 | tf_op jit(solution)/shard_map/all_to_all | solution.py:74
  166.3 51.9 %all-to-all-done.2 = bf16[32,2,16,400]{3,2,1,0:T(8,128)(2,1)S(1)} async-done(((bf16[32,2,16,400]{3,2,1,0:T(8,128)(2,1)}), bf16[32,2,16,400]{3,2,1,0:T(8,128)(2,1)S(1)}, u32[]{:S(2)}, u32[]{:S(2)}) %all-to-all-start.2) | async-done | bytes 819232 | tf_op jit(solution)/shard_map/all_to_all | solution.py:74
  218.4 2.6 collective-permute-start.2
  221.0 11.5 %collective-permute-done.2 = bf16[512,400]{1,0:T(8,128)(2,1)S(1)} collective-permute-done((bf16[512,400]{1,0:T(8,128)(2,1)S(1)}, bf16[512,400]{1,0:T(8,128)(2,1)S(1)}, u32[]{:S(2)}, u32[]{:S(2)}) %collective-permute-start.2) | collective-permute-done | bytes 409632 | tf_op jit(solution)/shard_map/ppermute | solution.py:14
  232.4 0.4 fusion.29
  232.8 0.4 fusion.53
  233.2 0.4 fusion.24
  233.6 0.3 add_multiply_fusion.1
  233.9 0.4 fusion.25
  234.3 0.3 add_convert_fusion
  234.6 0.7 pad_maximum_fusion.2
  235.4 0.3 fusion.28
  235.7 0.4 convolution_add_fusion.4
  236.3 2.8 collective-permute-start.3
  239.1 0.3 fusion.30
  239.5 0.4 convolution_add_fusion.5
  239.8 0.2 fusion.4
  240.3 6.8 %collective-permute-done.3 = bf16[512,400]{0,1:T(8,128)(2,1)S(1)} collective-permute-done((bf16[512,400]{0,1:T(8,128)(2,1)S(1)}, bf16[512,400]{0,1:T(8,128)(2,1)S(1)}, u32[]{:S(2)}, u32[]{:S(2)}) %collective-permute-start.3) | collective-permute-done | bytes 409632 | tf_op jit(solution)/shard_map/ppermute | solution.py:14
  247.4 1.1 copy.51
  248.5 11.0 %all-to-all-start.3 = ((bf16[32,2,16,400]{3,2,1,0:T(8,128)(2,1)}), bf16[32,2,16,400]{3,2,1,0:T(8,128)(2,1)S(1)}, u32[]{:S(2)}, u32[]{:S(2)}) async-start(bf16[32,2,16,400]{3,2,1,0:T(8,128)(2,1)} %copy.51), calls=%async_computation.3 | async-start | bytes 2097152 | tf_op jit(solution)/shard_map/all_to_all | solution.py:85
  259.5 15.7 %all-gather = s32[16,1,256]{2,1,0:T(1,128)S(1)} all-gather(s32[1,1,256]{2,1,0:T(1,128)S(1)} %bitcast.82), channel_id=1, replica_groups=mesh['dom'=16,'shard'=32] {'dom'}, dimensions={0}, use_global_device_ids=true | all-gather | bytes 17408 | tf_op jit(solution)/shard_map/all_gather | solution.py:90
  275.2 5.1 %all-gather.3.cloned.1.call-done = bf16[4096,400]{0,1:T(8,128)(2,1)} async-done(((bf16[256,400]{0,1:T(8,128)(2,1)}), bf16[4096,400]{0,1:T(8,128)(2,1)}) %all-gather.3.cloned.1.call-update) | async-done | bytes 3276816 | tf_op jit(solution)/shard_map/all_gather | solution.py:91
  280.3 3.0 fusion
  283.4 1.3 reshape.122
  284.7 26.2 %all-to-all-done.3 = bf16[32,2,16,400]{3,2,1,0:T(8,128)(2,1)S(1)} async-done(((bf16[32,2,16,400]{3,2,1,0:T(8,128)(2,1)}), bf16[32,2,16,400]{3,2,1,0:T(8,128)(2,1)S(1)}, u32[]{:S(2)}, u32[]{:S(2)}) %all-to-all-start.3) | async-done | bytes 819232 | tf_op jit(solution)/shard_map/all_to_all | solution.py:85
  310.9 7.4 %all-to-all-start.4 = ((f32[32,1,2000]{2,1,0:T(1,128)}), f32[32,1,2000]{2,1,0:T(1,128)S(1)}, u32[]{:S(2)}, u32[]{:S(2)}) async-start(f32[32,1,2000]{2,1,0:T(1,128)} %reshape.122), calls=%async_computation.4 | async-start | bytes 524288 | tf_op jit(solution)/shard_map/all_to_all | solution.py:96
  318.3 0.6 multiply_reduce_fusion.2
  318.9 0.5 fusion.66
  319.4 0.8 divide_subtract_fusion
  320.1 21.2 %all-to-all-done.4 = f32[32,1,2000]{2,1,0:T(1,128)S(1)} async-done(((f32[32,1,2000]{2,1,0:T(1,128)}), f32[32,1,2000]{2,1,0:T(1,128)S(1)}, u32[]{:S(2)}, u32[]{:S(2)}) %all-to-all-start.4) | async-done | bytes 256032 | tf_op jit(solution)/shard_map/all_to_all | solution.py:96
  341.3 0.5 broadcast.114
  341.8 1.3 reduce
  343.1 0.3 reshape.123
  343.6 0.5 fusion.65
  344.1 0.7 multiply_divide_fusion
  (54 shorter events, 3.3 us)
Async XLA Ops:
  10.9 70.7 %all-to-all-start = ((bf16[32,2,16,400]{3,2,1,0:T(8,128)(2,1)}), bf16[32,2,16,400]{3,2,1,0:T(8,128)(2,1)}, u32[]{:S(2)}, u32[]{:S(2)}) async-start(bf16[32,2,16,400]{3,2,1,0:T(8,128)(2,1)} %bitcast.3), calls=%async_computation | async-start | bytes 2097152 | tf_op jit(solution)/shard_map/all_to_all | solution.py:74
  29.1 2.9 copy-start.1
  32.0 1.4 copy-start.2
  32.0 1.6 copy-start.3
  32.0 1.8 copy-start.4
  32.1 52.7 %copy-start.5 = (s32[2,128]{1,0:T(2,128)S(1)}, s32[2,128]{1,0:T(2,128)}, u32[]{:S(2)}) copy-start(s32[2,128]{1,0:T(2,128)} %param.15) | copy-start | bytes 3076
  82.8 3.8 %collective-permute-start = (bf16[512,400]{1,0:T(8,128)(2,1)S(1)}, bf16[512,400]{1,0:T(8,128)(2,1)S(1)}, u32[]{:S(2)}, u32[]{:S(2)}) collective-permute-start(bf16[512,400]{1,0:T(8,128)(2,1)S(1)} %bitcast.73), channel_id=1, source_target_pairs={{0,32},{32,0},{64,96},{96,64},{128,160},{160,128},{192,224},{224,1... | collective-permute-start | bytes 1228808 | tf_op jit(solution)/shard_map/ppermute | solution.py:14
  89.8 3.6 %collective-permute-start.1 = (bf16[512,400]{0,1:T(8,128)(2,1)S(1)}, bf16[512,400]{0,1:T(8,128)(2,1)S(1)}, u32[]{:S(2)}, u32[]{:S(2)}) collective-permute-start(bf16[512,400]{0,1:T(8,128)(2,1)S(1)} %fusion.3), channel_id=1, source_target_pairs={{0,32},{32,0},{64,96},{96,64},{128,160},{160,128},{192,224},{224,1... | collective-permute-start | bytes 1228808 | tf_op jit(solution)/shard_map/ppermute | solution.py:14
  93.8 62.1 %copy-start.6 = (f32[64]{0:T(128)S(1)}, f32[64]{0:T(128)}, u32[]{:S(2)}) copy-start(f32[64]{0:T(128)} %param.11) | copy-start | bytes 772
  93.8 62.1 %copy-start = (f32[64,400]{1,0:T(8,128)S(1)}, f32[64,400]{1,0:T(8,128)}, u32[]{:S(2)}) copy-start(f32[64,400]{1,0:T(8,128)} %param.10) | copy-start | bytes 307204
  94.8 60.5 %all-to-all-start.1 = ((bf16[32,2,16,400]{3,2,1,0:T(8,128)(2,1)}), bf16[32,2,16,400]{3,2,1,0:T(8,128)(2,1)S(1)}, u32[]{:S(2)}, u32[]{:S(2)}) async-start(bf16[32,2,16,400]{3,2,1,0:T(8,128)(2,1)} %copy.46), calls=%async_computation.1 | async-start | bytes 2097152 | tf_op jit(solution)/shard_map/all_to_all | solution.py:85
  157.8 60.5 %all-to-all-start.2 = ((bf16[32,2,16,400]{3,2,1,0:T(8,128)(2,1)}), bf16[32,2,16,400]{3,2,1,0:T(8,128)(2,1)S(1)}, u32[]{:S(2)}, u32[]{:S(2)}) async-start(bf16[32,2,16,400]{3,2,1,0:T(8,128)(2,1)} %bitcast.13), calls=%async_computation.2 | async-start | bytes 2097152 | tf_op jit(solution)/shard_map/all_to_all | solution.py:74
  165.9 114.4 %all-gather.3.cloned.1.call-start = ((), (), s32[]{:S(2)}) async-start(), calls=%async_computation.5 | async-start | bytes 3481600 | tf_op jit(solution)/shard_map/all_gather | solution.py:91
  218.4 14.1 %collective-permute-start.2 = (bf16[512,400]{1,0:T(8,128)(2,1)S(1)}, bf16[512,400]{1,0:T(8,128)(2,1)S(1)}, u32[]{:S(2)}, u32[]{:S(2)}) collective-permute-start(bf16[512,400]{1,0:T(8,128)(2,1)S(1)} %bitcast.74), channel_id=1, source_target_pairs={{0,64},{32,96},{64,0},{96,32},{128,192},{160,224},{192,128},{224,1... | collective-permute-start | bytes 1228808 | tf_op jit(solution)/shard_map/ppermute | solution.py:14
  236.3 10.8 %collective-permute-start.3 = (bf16[512,400]{0,1:T(8,128)(2,1)S(1)}, bf16[512,400]{0,1:T(8,128)(2,1)S(1)}, u32[]{:S(2)}, u32[]{:S(2)}) collective-permute-start(bf16[512,400]{0,1:T(8,128)(2,1)S(1)} %fusion.5), channel_id=1, source_target_pairs={{0,64},{32,96},{64,0},{96,32},{128,192},{160,224},{192,128},{224,1... | collective-permute-start | bytes 1228808 | tf_op jit(solution)/shard_map/ppermute | solution.py:14
  248.5 62.3 %all-to-all-start.3 = ((bf16[32,2,16,400]{3,2,1,0:T(8,128)(2,1)}), bf16[32,2,16,400]{3,2,1,0:T(8,128)(2,1)S(1)}, u32[]{:S(2)}, u32[]{:S(2)}) async-start(bf16[32,2,16,400]{3,2,1,0:T(8,128)(2,1)} %copy.51), calls=%async_computation.3 | async-start | bytes 2097152 | tf_op jit(solution)/shard_map/all_to_all | solution.py:85
  283.4 60.2 %copy-start.7 = (f32[5]{0:T(128)S(1)}, f32[5]{0:T(128)}, u32[]{:S(2)}) copy-start(f32[5]{0:T(128)} %param.13) | copy-start | bytes 64
  310.9 30.5 %all-to-all-start.4 = ((f32[32,1,2000]{2,1,0:T(1,128)}), f32[32,1,2000]{2,1,0:T(1,128)S(1)}, u32[]{:S(2)}, u32[]{:S(2)}) async-start(f32[32,1,2000]{2,1,0:T(1,128)} %reshape.122), calls=%async_computation.4 | async-start | bytes 524288 | tf_op jit(solution)/shard_map/all_to_all | solution.py:96
Sparse Core Ops, SparseCore 0:
  235.5 44.7 all-gather.2

commit v2 on v1

--- a/solution.py
+++ b/solution.py
@@ -1,17 +1,19 @@
+import functools
+
 import jax
 import jax.numpy as jnp
 from jax import lax
+from jax.experimental import pallas as pl
+from jax.experimental.pallas import tpu as pltpu
 from jax.sharding import PartitionSpec as P
 
 LEARN_RATE = 0.1
 BF = jnp.bfloat16
 F32 = jnp.float32
-
-
-def partner(value, axis, distance):
-    mask = 2**distance
-    pairs = [(source, source ^ mask) for source in range(lax.axis_size(axis))]
-    return lax.ppermute(value, axis, pairs)
+MESH = pl.DeviceIdType.MESH
+WIDE = 512
+IDX_AT = 448
+PER = 64
 
 
 def mm(a, b, ca, cb):
@@ -26,6 +28,236 @@
     hi = b.astype(BF)
     lo = (b - hi.astype(F32)).astype(BF)
     return mm(a, hi, ca, cb) + mm(a, lo, ca, cb)
+
+
+def places(zs, mask):
+    g = lax.axis_index("dom")
+    s = lax.axis_index("shard")
+    z = lax.rem(s, zs)
+    yh = s // zs
+    h = jnp.bitwise_xor(g, mask)
+    base = yh * zs
+    other = (1 - yh) * zs
+    right = (g, base + lax.rem(z + 1, zs))
+    left = (g, base + lax.rem(z + zs - 1, zs))
+    peers = ((g, other + z), (h, s), (h, other + z))
+    return z, yh, right, left, peers
+
+
+def greet(devices):
+    barrier = pltpu.get_barrier_semaphore()
+    for device in devices:
+        pl.semaphore_signal(barrier, inc=1, device_id=device, device_id_type=MESH)
+    pl.semaphore_wait(barrier, len(devices))
+
+
+def hops(zs):
+    return ((zs // 2, zs - 1 - zs // 2), (zs - 1 - zs // 2, zs // 2))
+
+
+def remote(src, dst, send, recv, device):
+    return pltpu.make_async_remote_copy(
+        src_ref=src, dst_ref=dst, send_sem=send, recv_sem=recv, device_id=device, device_id_type=MESH
+    )
+
+
+def half(ref, d, c):
+    return ref.at[d, pl.ds(c * (PER // 2), PER // 2)]
+
+
+def gather_kernel(zs, slot, mask, block_ref, own_ref, far_ref, idx_ref, line, picked, ring_send, ring_recv, peer_send, peer_recv, self_sem):
+    z, yh, right, left, peers = places(zs, mask)
+    greet((right, left) + peers)
+    far_hops = hops(zs)
+
+    def ring(direction, t, c):
+        sign = -1 if direction == 0 else 1
+        d_src = (sign * (t - 1)) % zs
+        d_dst = (sign * t) % zs
+        src = block_ref.at[pl.ds(c * (PER // 2), PER // 2)] if t == 1 else half(line, d_src, c)
+        return remote(src, half(line, d_dst, c), ring_send.at[direction, t - 1, c], ring_recv.at[direction, t - 1, c], right if direction == 0 else left)
+
+    outgoing = []
+
+    def select(d):
+        block = block_ref[...] if d == 0 else line[d]
+        table = block[: zs if zs >= 16 else 16, WIDE - 128 :].astype(F32)
+        rows = lax.broadcasted_iota(jnp.int32, table.shape, 0)
+        ids = jnp.sum(jnp.where(rows == z, table, 0.0), axis=0, keepdims=True)
+        idx_ref[d : d + 1, :] = ids
+        ids = ids[:, IDX_AT - (WIDE - 128) :].astype(jnp.int32)
+        hot = (lax.broadcasted_iota(jnp.int32, (PER, PER), 0) == ids).astype(BF)
+        picked[d] = mm(hot, block, 0, 0).astype(BF)
+        owner = yh * zs + lax.rem(z + d, zs)
+        at = pl.ds(pl.multiple_of(owner * slot, slot), slot)
+        mine = yh * 2 * slot
+        theirs = (1 - yh) * 2 * slot
+        own_copy = pltpu.make_async_copy(picked.at[d, pl.ds(mine, slot)], own_ref.at[at], self_sem)
+        own_copy.start()
+        for k, (start, dst) in enumerate(((theirs, own_ref), (mine + slot, far_ref), (theirs + slot, far_ref))):
+            copy = remote(picked.at[d, pl.ds(start, slot)], dst.at[at], peer_send.at[k], peer_recv.at[k], peers[k])
+            copy.start()
+
+    for c in range(2):
+        for direction in range(2):
+            if far_hops[c][direction] >= 1:
+                ring(direction, 1, c).start()
+    select(0)
+    for t in range(1, zs // 2 + 1):
+        for c in range(2):
+            for direction in range(2):
+                if t <= far_hops[c][direction]:
+                    ring(direction, t, c).wait_recv()
+                    if t + 1 <= far_hops[c][direction]:
+                        ring(direction, t + 1, c).start()
+        select(zs - t)
+        if t != zs // 2:
+            select(t)
+    for t in range(1, zs // 2 + 1):
+        for c in range(2):
+            for direction in range(2):
+                if t <= far_hops[c][direction]:
+                    ring(direction, t, c).wait_send()
+    total = zs * slot
+    whole = own_ref.at[pl.ds(0, total)]
+    pltpu.make_async_copy(whole, whole, self_sem).wait()
+    for k in range(3):
+        copy = remote(whole, whole, peer_send.at[k], peer_recv.at[k], peers[k])
+        copy.wait_send()
+        copy.wait_recv()
+
+
+def scatter_kernel(zs, slot, mask, own_ref, far_ref, idx_ref, grad_ref, got, term, sent, came, ring_send, ring_recv, peer_send, peer_recv, self_sem):
+    z, yh, right, left, peers = places(zs, mask)
+    greet((right, left) + peers)
+    far_hops = hops(zs)
+    mine = yh * 2 * slot
+    theirs = (1 - yh) * 2 * slot
+
+    def rows_of(line_yh, d):
+        owner = line_yh * zs + lax.rem(z + d, zs)
+        return pl.ds(pl.multiple_of(owner * slot, slot), slot)
+
+    def exchange(d):
+        return (
+            pltpu.make_async_copy(own_ref.at[rows_of(yh, d)], got.at[d, pl.ds(mine, slot)], self_sem.at[d]),
+            remote(own_ref.at[rows_of(1 - yh, d)], got.at[d, pl.ds(mine, slot)], peer_send.at[0], peer_recv.at[d, 0], peers[0]),
+            remote(far_ref.at[rows_of(yh, d)], got.at[d, pl.ds(mine + slot, slot)], peer_send.at[1], peer_recv.at[d, 1], peers[1]),
+            remote(far_ref.at[rows_of(1 - yh, d)], got.at[d, pl.ds(mine + slot, slot)], peer_send.at[2], peer_recv.at[d, 2], peers[2]),
+        )
+
+    order = []
+    for t in range(zs // 2, 0, -1):
+        order.append(t)
+        if t != zs // 2:
+            order.append(zs - t)
+    order.append(0)
+    for d in order:
+        for copy in exchange(d):
+            copy.start()
+
+    def make_term(d):
+        copies = exchange(d)
+        copies[0].wait()
+        for copy in copies[1:]:
+            copy.wait_recv()
+        ids = idx_ref[d : d + 1, IDX_AT - (WIDE - 128) :].astype(jnp.int32)
+        hot = (lax.broadcasted_iota(jnp.int32, (PER, PER), 0) == ids).astype(BF)
+        term[d] = mm(hot, got[d], 1, 0)
+
+    def ring(direction, t, c):
+        return remote(sent.at[direction, t - 1, c], came.at[direction, t - 1, c], ring_send.at[direction, t - 1, c], ring_recv.at[direction, t - 1, c], right if direction == 0 else left)
+
+    made = set()
+    for t in range(1, zs // 2 + 1):
+        for c in range(2):
+            for direction in range(2):
+                count = far_hops[c][direction]
+                if t > count:
+                    continue
+                d = count - t + 1
+                d = d % zs if direction == 0 else (-d) % zs
+                if d not in made:
+                    make_term(d)
+                    made.add(d)
+                value = term[d, pl.ds(c * (PER // 2), PER // 2)]
+                if t > 1:
+                    ring(direction, t - 1, c).wait_recv()
+                    value = value + came[direction, t - 2, c].astype(F32)
+                sent[direction, t - 1, c] = value.astype(BF)
+                ring(direction, t, c).start()
+    make_term(0)
+    for c in range(2):
+        at = pl.ds(c * (PER // 2), PER // 2)
+        value = term[0, at]
+        for direction in range(2):
+            count = far_hops[c][direction]
+            if count:
+                ring(direction, count, c).wait_recv()
+                value = value + came[direction, count - 1, c].astype(F32)
+        grad_ref[at, :] = value
+    for t in range(1, zs // 2 + 1):
+        for c in range(2):
+            for direction in range(2):
+                if t <= far_hops[c][direction]:
+                    ring(direction, t, c).wait_send()
+    whole = own_ref.at[pl.ds(0, zs * slot)]
+    for k in range(3):
+        remote(whole, whole, peer_send.at[k], peer_recv.at[0, k], peers[k]).wait_send()
+
+
+VMEM_SPEC = pl.BlockSpec(memory_space=pltpu.VMEM)
+
+
+def fetch(block, zs, slot, mask, cid):
+    touch = 2 * zs * slot
+    steps = zs // 2
+    dma = pltpu.SemaphoreType.DMA
+    return pl.pallas_call(
+        functools.partial(gather_kernel, zs, slot, mask),
+        name="fetch_rows",
+        out_shape=(
+            jax.ShapeDtypeStruct((touch, WIDE), BF),
+            jax.ShapeDtypeStruct((touch, WIDE), BF),
+            jax.ShapeDtypeStruct((zs, 128), F32),
+        ),
+        in_specs=[VMEM_SPEC],
+        out_specs=(VMEM_SPEC,) * 3,
+        scratch_shapes=[
+            pltpu.VMEM((zs, PER, WIDE), BF),
+            pltpu.VMEM((zs, PER, WIDE), BF),
+            dma((2, steps, 2)),
+            dma((2, steps, 2)),
+            dma((3,)),
+            dma((3,)),
+            dma,
+        ],
+        compiler_params=pltpu.CompilerParams(collective_id=cid, has_side_effects=True),
+    )(block)
+
+
+def give_back(own_grad, far_grad, idx, zs, slot, mask, cid):
+    steps = zs // 2
+    dma = pltpu.SemaphoreType.DMA
+    return pl.pallas_call(
+        functools.partial(scatter_kernel, zs, slot, mask),
+        name="return_grads",
+        out_shape=jax.ShapeDtypeStruct((PER, WIDE), F32),
+        in_specs=[VMEM_SPEC] * 3,
+        out_specs=VMEM_SPEC,
+        scratch_shapes=[
+            pltpu.VMEM((zs, PER, WIDE), BF),
+            pltpu.VMEM((zs, PER, WIDE), F32),
+            pltpu.VMEM((2, steps, 2, PER // 2, WIDE), BF),
+            pltpu.VMEM((2, steps, 2, PER // 2, WIDE), BF),
+            dma((2, steps, 2)),
+            dma((2, steps, 2)),
+            dma((3,)),
+            dma((zs, 3)),
+            dma((zs,)),
+        ],
+        compiler_params=pltpu.CompilerParams(collective_id=cid, has_side_effects=True),
+    )(own_grad, far_grad, idx)
 
 
 def edge_terms(own, far, head_slots, tail_slots, rel_vec, own_neg, far_neg):
@@ -59,31 +291,24 @@
 def body(embeddings, row_accum, relations, relation_accum, request_rows, head_slots, tail_slots, relation_ids, own_negatives, far_negatives):
     rows, width = embeddings.shape
     shards = lax.axis_size("shard")
-    slot_count = request_rows.shape[-1]
-    touch = shards * slot_count
+    slot = request_rows.shape[-1]
+    zs = shards // 2
     rounds = request_rows.shape[0]
     emb = embeddings
     accum = row_accum
     rel_rows = []
     all_rel = relations[relation_ids.reshape(-1)].astype(F32).reshape(rounds, -1, width)
+    all_rel = jnp.pad(all_rel, ((0, 0), (0, 0), (0, WIDE - width)))
+    wanted = request_rows.reshape(rounds, 2, zs, 2 * slot).transpose(0, 2, 1, 3).reshape(rounds, zs, 4 * slot)
+    wanted = jnp.pad(wanted, ((0, 0), (0, rows - zs), (IDX_AT - width, 0))).astype(BF)
     for r in range(rounds):
-        lowered = emb.astype(BF)
-        ids = request_rows[r].reshape(-1)
-        hot = one_hot(ids, rows)
-        served = mm(hot, lowered, 1, 0).astype(BF).reshape(shards, 2, slot_count, width)
-        received = lax.all_to_all(served, "shard", split_axis=0, concat_axis=0, tiled=True)
-        own = received[:, 0].reshape(touch, width)
-        far = partner(received[:, 1].reshape(touch, width), "dom", r)
+        block = jnp.concatenate([emb.astype(BF), wanted[r]], axis=1)
+        own, far, idx = fetch(block, zs, slot, 1 << r, 2 * r)
         own_grad, far_grad, grad_rel = edge_terms(
             own, far, head_slots[r], tail_slots[r], all_rel[r], own_negatives[r], far_negatives[r]
         )
-        rel_rows.append(grad_rel.astype(BF))
-        far_back = partner(far_grad, "dom", r)
-        outgoing = jnp.stack(
-            [own_grad.reshape(shards, slot_count, width), far_back.reshape(shards, slot_count, width)], axis=1
-        )
-        returned = lax.all_to_all(outgoing, "shard", split_axis=0, concat_axis=0, tiled=True)
-        row_grad = mm(hot, returned.reshape(-1, width), 0, 0)
+        rel_rows.append(grad_rel[:, :width].astype(BF))
+        row_grad = give_back(own_grad, far_grad, idx, zs, slot, 1 << r, 2 * r + 1)[:, :width]
         accum = accum + jnp.mean(row_grad * row_grad, axis=-1)
         emb = emb - LEARN_RATE * row_grad / jnp.sqrt(accum)[:, None]
     mine = jnp.concatenate(rel_rows, axis=0)

time: 353 us -> 272 us (0.77)
  waiting for transfers between devices: 225 us -> 20.5 us
  Pallas kernels: 0 us -> 161 us
  starting transfers between devices: 62.1 us -> 14.9 us
  other arithmetic: 5.68 us -> 12.8 us
  matrix products: 14.3 us -> 20.9 us
  local copies, waits for them, and re-layouts: 14.4 us -> 9.63 us
    all_to_all x4 -> x0, waiting for transfers between devices: 178 us -> none  [the longest x2 99.6 us: body(): lax.all_to_all(served, 'shard', split_axis=0, concat_axis=0, tiled=True)]
    pallas_call x0 -> x4, Pallas kernels: none -> 161 us  [the longest x2 80.6 us: give_back(): pl.pallas_call(functools.partial(scatter_kernel, zs, slot, mask), name='r...]
    all_to_all x4 -> x0, starting transfers between devices: 45.3 us -> none  [the longest x2 26.4 us: body(): lax.all_to_all(served, 'shard', split_axis=0, concat_axis=0, tiled=True)]
    all_to_all x1, waiting for transfers between devices: 21.2 us -> 0.01 us  [body(): lax.all_to_all(pieces, 'shard', split_axis=0, concat_axis=0, tiled=True)]
    ppermute x4 -> x0, waiting for transfers between devices: 20.5 us -> none  [partner(): return lax.ppermute(value, axis, pairs)]
    all_gather x1, waiting for transfers between devices: 5.08 us -> 20.5 us  [body(): group_rows = lax.all_gather(mine, 'dom', tiled=True)]
    ppermute x4 -> x0, starting transfers between devices: 9.33 us -> none  [partner(): return lax.ppermute(value, axis, pairs)]
    all_to_all x1, starting transfers between devices: 7.43 us -> 14.8 us  [body(): lax.all_to_all(pieces, 'shard', split_axis=0, concat_axis=0, tiled=True)]
  transfers between devices with their start and end apart: 10 -> 2, of which waited for: 10 -> 1; matrix products, arithmetic and copies ran while one was open for 5% -> 3% of each run, Pallas kernels for 0% -> 16%
where the time goes in v2:
time: 272 us; the launch traced here: 270 us
  Pallas kernels  161 us (59%)
  matrix products  20.9 us (8%)
  waiting for transfers between devices  20.5 us (8%)
  blocking collectives  15.8 us (6%)
  starting transfers between devices  14.9 us (5%)
  between operations  14.7 us (5%)
  other arithmetic  12.8 us (5%)
  local copies, waits for them, and re-layouts  9.63 us (4%)
    pallas_call x2, Pallas kernels, give_back(): pl.pallas_call(functools.partial(scatter_kernel, zs, slot, mask), name='r...  80.6 us
    pallas_call x2, Pallas kernels, fetch(): pl.pallas_call(functools.partial(gather_kernel, zs, slot, mask), name='fe...  80.1 us
    dot_general x25, matrix products, mm(): lax.dot_general(a, b, (((ca,), (cb,)), ((), ())), preferred_element_type=...  20.9 us
    all_gather x1, waiting for transfers between devices, body(): group_rows = lax.all_gather(mine, 'dom', tiled=True)  20.5 us
    all_gather x1, blocking collectives, body(): ids = lax.all_gather(relation_ids.reshape(-1), 'dom', tiled=True)  15.8 us
    all_to_all x1, starting transfers between devices, body(): lax.all_to_all(pieces, 'shard', split_axis=0, concat_axis=0, tiled=True)  14.8 us
  transfers between devices with their start and end apart: 2, of which 1 were waited for; matrix products, arithmetic and copies ran while one was open for 3% of the time, Pallas kernels for 16%

profile of v2, /device:TPU:6, one launch (start us, length us, event | category | flops | bytes accessed | tf_op | source)
XLA Modules:
  0.0 269.9 jit_solution(17362825725421296812)
XLA Ops:
  7.2 1.3 slice_bitcast_fusion.5
  8.5 0.8 convert.16
  9.2 0.1 reshape.113
  9.3 0.1 copy.25
  9.4 0.1 reshape.97
  9.5 0.1 fusion.64
  9.6 0.9 convert_element_type.106
  10.5 0.7 pad_maximum_fusion.1.block_ref
  11.2 44.2 %fetch_rows.2 = (bf16[512,512]{1,0:T(8,128)(2,1)}, bf16[512,512]{1,0:T(8,128)(2,1)}, f32[16,128]{1,0:T(8,128)}) custom-call(bf16[64,512]{1,0:T(8,128)(2,1)} %pad_maximum_fusion.1.block_ref), custom_call_target="tpu_custom_call" | custom-call | tf_op jit(solution)/shard_map/fetch_rows/pallas_call | solution.py:216
  55.4 2.9 %copy.22 = bf16[2560,400]{1,0:T(8,128)(2,1)S(1)} copy(bf16[2560,400]{0,1:T(8,128)(2,1)} %param.12) | data formatting | bytes 4096000 | tf_op args[2]
  58.4 1.2 gather_fusion
  59.6 1.3 fusion.39
  60.9 0.4 multiply_reduce_fusion.1
  61.3 0.2 convert_reduce_fusion.3
  61.5 0.4 fusion.25
  61.9 0.9 multiply_convert_fusion.1
  62.9 0.4 fusion.38
  63.3 0.4 convolution_add_fusion.7
  63.7 0.2 convert_reduce_fusion.2
  63.9 0.3 fusion.24
  64.3 0.2 fusion.72
  64.5 1.1 fusion.2.own_ref
  65.6 0.4 fusion.36
  66.1 0.4 convolution_add_fusion.5
  66.5 1.1 fusion.3.far_ref
  67.6 37.5 %return_grads.2 = f32[64,512]{1,0:T(8,128)} custom-call(bf16[512,512]{1,0:T(8,128)(2,1)} %fusion.2.own_ref, bf16[512,512]{1,0:T(8,128)(2,1)} %fusion.3.far_ref, f32[16,128]{1,0:T(8,128)} %get-tuple-element.12.idx_ref), custom_call_target="tpu_custom_call" | custom-call | tf_op jit(solution)/shard_map/return_grads/pallas_call | solution.py:242
  105.1 1.0 multiply_reduce_fusion.3
  106.2 1.0 fusion.67
  107.2 0.7 pad_maximum_fusion.2.block_ref
  107.9 35.9 %fetch_rows.3 = (bf16[512,512]{1,0:T(8,128)(2,1)}, bf16[512,512]{1,0:T(8,128)(2,1)}, f32[16,128]{1,0:T(8,128)}) custom-call(bf16[64,512]{1,0:T(8,128)(2,1)} %pad_maximum_fusion.2.block_ref), custom_call_target="tpu_custom_call" | custom-call | tf_op jit(solution)/shard_map/fetch_rows/pallas_call | solution.py:216
  143.9 1.4 fusion.35
  145.2 1.5 multiply_reduce_fusion
  146.7 0.2 convert_reduce_fusion.1
  146.9 0.2 convert_reduce_fusion
  147.1 1.4 fusion.23
  148.6 0.2 multiply_convert_fusion
  148.8 0.4 copy-done.9
  149.2 0.3 copy-done.11
  149.5 0.4 fusion.22
  149.9 0.2 fusion.73
  150.1 0.3 fusion.27
  150.4 0.7 pad_maximum_fusion
  151.2 15.8 %all-gather = s32[16,1,256]{2,1,0:T(1,128)S(1)} all-gather(s32[1,1,256]{2,1,0:T(1,128)S(1)} %bitcast.106), channel_id=1, replica_groups=mesh['dom'=16,'shard'=32] {'dom'}, dimensions={0}, use_global_device_ids=true | all-gather | bytes 17408 | tf_op jit(solution)/shard_map/all_gather | solution.py:315
  167.0 0.4 fusion.34
  167.4 0.4 fusion.32
  167.9 1.1 convolution_add_fusion.3
  168.9 0.4 convolution_add_fusion.1
  169.4 20.5 %all-gather.3.cloned.1.call-done = bf16[4096,400]{1,0:T(8,128)(2,1)} async-done(((bf16[256,400]{1,0:T(8,128)(2,1)}), bf16[4096,400]{1,0:T(8,128)(2,1)}) %all-gather.3.cloned.1.call-update) | async-done | bytes 3276816 | tf_op jit(solution)/shard_map/all_gather | solution.py:316
  189.9 3.8 %fusion = f32[160,400]{1,0:T(8,128)} fusion(bf16[4096,400]{1,0:T(8,128)(2,1)} %all-gather.3.cloned.1.call-done, s32[4096]{0:T(1024)S(1)} %bitcast.100), kind=kOutput, calls=%fused_computation.2 | convolution fusion | flops 524943360 | bytes 3549184 | tf_op jit(solution)/shard_map/dot_general | solution.py:20
  193.7 1.1 reshape.99
  194.8 1.3 reshape.114
  196.0 14.8 %all-to-all-start = ((f32[32,1,2000]{2,1,0:T(1,128)}), f32[32,1,2000]{2,1,0:T(1,128)S(1)}, u32[]{:S(2)}, u32[]{:S(2)}) async-start(f32[32,1,2000]{2,1,0:T(1,128)} %reshape.114), calls=%async_computation | async-start | bytes 524288 | tf_op jit(solution)/shard_map/all_to_all | solution.py:321
  210.9 1.1 fusion.4.own_ref
  212.1 1.1 fusion.5.far_ref
  213.2 43.1 %return_grads.3 = f32[64,512]{1,0:T(8,128)} custom-call(bf16[512,512]{1,0:T(8,128)(2,1)} %fusion.4.own_ref, bf16[512,512]{1,0:T(8,128)(2,1)} %fusion.5.far_ref, f32[16,128]{1,0:T(8,128)} %get-tuple-element.15.idx_ref), custom_call_target="tpu_custom_call" | custom-call | tf_op jit(solution)/shard_map/return_grads/pallas_call | solution.py:242
  256.3 1.0 multiply_reduce_fusion.2
  257.3 0.5 fusion.69
  257.9 1.7 divide_subtract_fusion
  259.5 0.5 broadcast.117
  260.0 1.3 reduce
  261.3 0.3 reshape.115
  261.7 0.1 multiply_reduce_fusion.4
  261.8 0.5 fusion.68
  262.3 0.7 multiply_divide_fusion
  (81 shorter events, 0.4 us)
Async XLA Ops:
  7.2 182.7 %all-gather.3.cloned.1.call-start = ((), (), s32[]{:S(2)}) async-start(), calls=%async_computation.1 | async-start | bytes 4456448 | tf_op jit(solution)/shard_map/all_gather | solution.py:316
  9.3 49.0 %copy-start.20 = (s32[2,128]{1,0:T(2,128)S(1)}, s32[2,128]{1,0:T(2,128)}, u32[]{:S(2)}) copy-start(s32[2,128]{1,0:T(2,128)} %param.17) | copy-start | bytes 3076
  58.3 1.3 copy-start.28
  58.3 2.6 copy-start
  58.4 3.0 %copy-start.22 = (s32[2,512]{1,0:T(2,128)S(1)}, s32[2,512]{1,0:T(2,128)}, u32[]{:S(2)}) copy-start(s32[2,512]{1,0:T(2,128)} %param.19) | copy-start | bytes 12292
  59.6 85.6 %copy-start.17 = (s32[128]{0:T(128)}, s32[128]{0:T(128)S(1)}, u32[]{:S(2)}) copy-start(s32[128]{0:T(128)S(1)} %get-tuple-element.34) | copy-start | bytes 1540
  61.9 1.8 copy-start.23
  61.9 2.0 copy-start.2
  66.1 40.1 %copy-start.29 = (f32[64]{0:T(128)S(1)}, f32[64]{0:T(128)}, u32[]{:S(2)}) copy-start(f32[64]{0:T(128)} %param.11) | copy-start | bytes 772
  66.1 40.1 %copy-start.5 = (f32[64,400]{1,0:T(8,128)S(1)}, f32[64,400]{1,0:T(8,128)}, u32[]{:S(2)}) copy-start(f32[64,400]{1,0:T(8,128)} %param.10) | copy-start | bytes 307204
  66.1 77.8 %copy-start.15 = (s32[128]{0:T(128)S(1)}, s32[128]{0:T(128)}, u32[]{:S(2)}) copy-start(s32[128]{0:T(128)} %get-tuple-element.37) | copy-start | bytes 1540
  106.1 42.4 %copy-start.24 = (f32[64]{0:T(128)}, f32[64]{0:T(128)S(1)}, u32[]{:S(2)}) copy-start(f32[64]{0:T(128)S(1)} %multiply_reduce_fusion.3) | copy-start | bytes 772
  106.2 37.7 %copy-start.26 = (f32[64]{0:T(128)}, f32[64]{0:T(128)S(1)}, u32[]{:S(2)}) copy-start(f32[64]{0:T(128)S(1)} %fusion.66) | copy-start | bytes 772
  143.8 4.7 %copy-start.1 = (bf16[512,512]{1,0:T(8,128)(2,1)S(1)}, bf16[512,512]{1,0:T(8,128)(2,1)}, u32[]{:S(2)}) copy-start(bf16[512,512]{1,0:T(8,128)(2,1)} %get-tuple-element.14) | copy-start | bytes 1572868
  145.2 4.2 %copy-start.3 = (bf16[512,512]{1,0:T(8,128)(2,1)S(1)}, bf16[512,512]{1,0:T(8,128)(2,1)}, u32[]{:S(2)}) copy-start(bf16[512,512]{1,0:T(8,128)(2,1)} %get-tuple-element.13) | copy-start | bytes 1572868
  146.7 1.8 copy-start.7
  148.5 0.7 copy-start.9
  148.5 1.6 copy-start.6
  148.8 0.7 copy-start.11
  149.8 17.6 %copy-start.13 = (bf16[128,512]{1,0:T(8,128)(2,1)}, bf16[128,512]{1,0:T(8,128)(2,1)S(1)}, u32[]{:S(2)}) copy-start(bf16[128,512]{1,0:T(8,128)(2,1)S(1)} %fusion.22) | copy-start | bytes 393220
  149.8 1.4 copy-start.21
  149.9 17.1 %copy-start.16 = (s32[128]{0:T(128)S(1)}, s32[128]{0:T(128)}, u32[]{:S(2)}) copy-start(s32[128]{0:T(128)} %get-tuple-element.37) | copy-start | bytes 1540
  150.1 17.3 %copy-start.18 = (s32[128]{0:T(128)S(1)}, s32[128]{0:T(128)}, u32[]{:S(2)}) copy-start(s32[128]{0:T(128)} %copy-done.17) | copy-start | bytes 1540
  167.0 1.9 copy-start.19
  189.9 21.0 %copy-start.12 = (bf16[128,512]{1,0:T(8,128)(2,1)S(1)}, bf16[128,512]{1,0:T(8,128)(2,1)}, u32[]{:S(2)}) copy-start(bf16[128,512]{1,0:T(8,128)(2,1)} %copy-done.11) | copy-start | bytes 393220
  189.9 21.0 %copy-start.14 = (bf16[128,512]{1,0:T(8,128)(2,1)S(1)}, bf16[128,512]{1,0:T(8,128)(2,1)}, u32[]{:S(2)}) copy-start(bf16[128,512]{1,0:T(8,128)(2,1)} %copy-done.13) | copy-start | bytes 393220
  193.7 18.4 %copy-start.8 = (bf16[128,512]{1,0:T(8,128)(2,1)S(1)}, bf16[128,512]{1,0:T(8,128)(2,1)}, u32[]{:S(2)}) copy-start(bf16[128,512]{1,0:T(8,128)(2,1)} %copy-done.7) | copy-start | bytes 393220
  193.7 18.4 %copy-start.10 = (bf16[128,512]{1,0:T(8,128)(2,1)S(1)}, bf16[128,512]{1,0:T(8,128)(2,1)}, u32[]{:S(2)}) copy-start(bf16[128,512]{1,0:T(8,128)(2,1)} %copy-done.9) | copy-start | bytes 393220
  196.0 63.5 %all-to-all-start = ((f32[32,1,2000]{2,1,0:T(1,128)}), f32[32,1,2000]{2,1,0:T(1,128)S(1)}, u32[]{:S(2)}, u32[]{:S(2)}) async-start(f32[32,1,2000]{2,1,0:T(1,128)} %reshape.114), calls=%async_computation | async-start | bytes 524288 | tf_op jit(solution)/shard_map/all_to_all | solution.py:321
  210.9 46.4 %copy-start.25 = (f32[64]{0:T(128)S(1)}, f32[64]{0:T(128)}, u32[]{:S(2)}) copy-start(f32[64]{0:T(128)} %copy-done.24) | copy-start | bytes 772
  210.9 46.4 %copy-start.30 = (f32[64]{0:T(128)S(1)}, f32[64]{0:T(128)}, u32[]{:S(2)}) copy-start(f32[64]{0:T(128)} %param.11) | copy-start | bytes 772
  210.9 46.9 %copy-start.4 = (f32[64,512]{1,0:T(8,128)S(1)}, f32[64,512]{1,0:T(8,128)}, u32[]{:S(2)}) copy-start(f32[64,512]{1,0:T(8,128)} %return_grads.2) | copy-start | bytes 393220
  210.9 46.9 %copy-start.27 = (f32[64]{0:T(128)S(1)}, f32[64]{0:T(128)}, u32[]{:S(2)}) copy-start(f32[64]{0:T(128)} %copy-done.26) | copy-start | bytes 772
  212.1 49.7 %copy-start.31 = (f32[5]{0:T(128)S(1)}, f32[5]{0:T(128)}, u32[]{:S(2)}) copy-start(f32[5]{0:T(128)} %param.13) | copy-start | bytes 64
Sparse Core Ops, SparseCore 0:
  151.3 38.4 all-gather.2

commit v3 on v1

v3 whole, which is shorter than its diff:
```python
import functools

import jax
import jax.numpy as jnp
from jax import lax
from jax.experimental import pallas as pl
from jax.experimental.pallas import tpu as pltpu
from jax.sharding import PartitionSpec as P

LEARN_RATE = 0.1
BF = jnp.bfloat16
F32 = jnp.float32
I32 = jnp.int32
MESH = pl.DeviceIdType.MESH
WIDE = 512
TAIL = WIDE - 128
MARK = 64
PER = 64
HALF = PER // 2
RELS = 5
INNER = 4


def mm(a, b, ca, cb):
    return lax.dot_general(a, b, (((ca,), (cb,)), ((), ())), preferred_element_type=F32)


def iota(shape, dim):
    return lax.broadcasted_iota(I32, shape, dim)


def hops(zs):
    return ((zs // 2, zs - 1 - zs // 2), (zs - 1 - zs // 2, zs // 2))


def remote(src, dst, send, recv, device):
    return pltpu.make_async_remote_copy(
        src_ref=src, dst_ref=dst, send_sem=send, recv_sem=recv, device_id=device, device_id_type=MESH
    )


class Place:
    def __init__(self, zs, xs):
        self.zs, self.xs = zs, xs
        g = lax.axis_index("dom")
        s = lax.axis_index("shard")
        self.g, self.s = g, s
        self.z = lax.rem(s, zs)
        self.yh = s // zs
        self.other = (1 - self.yh) * zs + self.z
        self.x = g // INNER
        self.inner = lax.rem(g, INNER)
        self.core = lax.rem(g, 2)
        self.ylo = self.inner // 2
        self.mate = g + 1 - 2 * self.core
        self.far_y = g + 2 - 4 * self.ylo

    def along_z(self, d):
        return (self.g, self.yh * self.zs + lax.rem(self.z + d, self.zs))

    def along_x(self, d):
        return (lax.rem(self.x + d, self.xs) * INNER + self.inner, self.s)

    def peers(self, r):
        h = self.mate if r == 0 else self.far_y
        return ((self.g, self.other), (h, self.s), (h, self.other))

    def everyone(self):
        return (
            [self.along_z(d) for d in range(1, self.zs)]
            + [self.along_x(d) for d in range(1, self.xs)]
            + list(self.peers(0))
            + list(self.peers(1)[1:])
        )

    def owner_rows(self, yh, d, slot):
        owner = yh * self.zs + lax.rem(self.z + d, self.zs)
        return pl.ds(pl.multiple_of(owner * slot, slot), slot)


class Ring:
    def __init__(self, place, send, recv):
        self.place, self.send, self.recv = place, send, recv
        self.count = hops(place.zs)

    def copy(self, src, dst, direction, t, c):
        return remote(
            src, dst, self.send.at[direction, t - 1, c], self.recv.at[direction, t - 1, c],
            self.place.along_z(1 if direction == 0 else self.place.zs - 1),
        )

    def each(self, t):
        for c in range(2):
            for direction in range(2):
                if t <= self.count[c][direction]:
                    yield direction, c


def piece(ref, c):
    return ref.at[pl.ds(c * HALF, HALF)]


def fetch(place, r, slot, block, line, picked, own, far, idx, ring, peer_send, peer_recv, self_sem, prepare):
    zs, peers = place.zs, place.peers(r)

    def step(direction, t, c):
        sign = -1 if direction == 0 else 1
        src = piece(block, c) if t == 1 else piece(line.at[(sign * (t - 1)) % zs], c)
        return ring.copy(src, piece(line.at[(sign * t) % zs], c), direction, t, c)

    def select(d):
        value = block[...] if d == 0 else line[d]
        table = value[:16, TAIL:].astype(F32)
        ids = jnp.sum(jnp.where(iota(table.shape, 0) == place.z, table, 0.0), axis=0, keepdims=True)
        idx[d : d + 1, :] = ids
        hot = (iota((PER, PER), 0) == ids[:, MARK:].astype(I32)).astype(BF)
        picked[d] = mm(hot, value, 0, 0).astype(BF)
        at = place.owner_rows(place.yh, d, slot)
        mine = place.yh * 2 * slot
        theirs = (1 - place.yh) * 2 * slot
        pltpu.make_async_copy(picked.at[d, pl.ds(mine, slot)], own.at[at], self_sem).start()
        for k, (start, dst) in enumerate(((theirs, own), (mine + slot, far), (theirs + slot, far))):
            remote(picked.at[d, pl.ds(start, slot)], dst.at[at], peer_send.at[k], peer_recv.at[k], peers[k]).start()

    for direction, c in ring.each(1):
        step(direction, 1, c).start()
    select(0)
    prepare()
    for t in range(1, zs // 2 + 1):
        for direction, c in ring.each(t):
            step(direction, t, c).wait_recv()
            if t + 1 <= ring.count[c][direction]:
                step(direction, t + 1, c).start()
        select(zs - t)
        if t != zs // 2:
            select(t)
    for t in range(1, zs // 2 + 1):
        for direction, c in ring.each(t):
            step(direction, t, c).wait_send()
    whole = own.at[pl.ds(0, zs * slot)]
    pltpu.make_async_copy(whole, whole, self_sem).wait()
    for k in range(3):
        copy = remote(whole, whole, peer_send.at[k], peer_recv.at[k], peers[k])
        copy.wait_send()
        copy.wait_recv()


def give_back(place, r, slot, own, far, idx, got, term, sent, came, ring, peer_send, peer_recv, self_sem, aside):
    zs, peers = place.zs, place.peers(r)
    mine = place.yh * 2 * slot

    def exchange(d):
        here, there = place.owner_rows(place.yh, d, slot), place.owner_rows(1 - place.yh, d, slot)
        k0, k1 = got.at[d, pl.ds(mine, slot)], got.at[d, pl.ds(mine + slot, slot)]
        return (
            pltpu.make_async_copy(own.at[here], k0, self_sem.at[d]),
            remote(own.at[there], k0, peer_send.at[0], peer_recv.at[d, 0], peers[0]),
            remote(far.at[here], k1, peer_send.at[1], peer_recv.at[d, 1], peers[1]),
            remote(far.at[there], k1, peer_send.at[2], peer_recv.at[d, 2], peers[2]),
        )

    def step(direction, t, c):
        return ring.copy(sent.at[direction, t - 1, c], came.at[direction, t - 1, c], direction, t, c)

    def make_term(d):
        copies = exchange(d)
        copies[0].wait()
        for copy in copies[1:]:
            copy.wait_recv()
        hot = (iota((PER, PER), 0) == idx[d : d + 1, MARK:].astype(I32)).astype(BF)
        term[d] = mm(hot, got[d], 1, 0)

    for t in range(zs // 2, 0, -1):
        for d in (t,) if t == zs // 2 else (t, zs - t):
            for copy in exchange(d):
                copy.start()
    for copy in exchange(0):
        copy.start()
    aside[0]()
    made = set()
    for t in range(1, zs // 2 + 1):
        for direction, c in ring.each(t):
            d = ring.count[c][direction] - t + 1
            d = d % zs if direction == 0 else (-d) % zs
            if d not in made:
                make_term(d)
                made.add(d)
            value = term[d, pl.ds(c * HALF, HALF)]
            if t > 1:
                step(direction, t - 1, c).wait_recv()
                value = value + came[direction, t - 2, c].astype(F32)
            sent[direction, t - 1, c] = value.astype(BF)
            step(direction, t, c).start()
        if t in aside:
            aside[t]()
    make_term(0)
    halves = []
    for c in range(2):
        value = term[0, pl.ds(c * HALF, HALF)]
        for direction in range(2):
            count = ring.count[c][direction]
            if count:
                step(direction, count, c).wait_recv()
                value = value + came[direction, count - 1, c].astype(F32)
        halves.append(value)
    for t in range(1, zs // 2 + 1):
        for direction, c in ring.each(t):
            step(direction, t, c).wait_send()
    whole = own.at[pl.ds(0, zs * slot)]
    for k in range(3):
        remote(whole, whole, peer_send.at[k], peer_recv.at[0, k], peers[k]).wait_send()
    return jnp.concatenate(halves, axis=0)


def main_kernel(zs, xs, slot, width, names, *refs):
    n = dict(zip(names, refs))
    place = Place(zs, xs)
    touch = 2 * zs * slot
    edges = n["edge_slots"].shape[1]
    nrel = n["rel_table"].shape[0]
    seg = zs * RELS

    table_copy = pltpu.make_async_copy(n["relations"], n["rel_table"], n["table_sem"])
    table_copy.start()
    barrier = pltpu.get_barrier_semaphore()
    everyone = place.everyone()
    for device in everyone:
        pl.semaphore_signal(barrier, inc=1, device_id=device, device_id_type=MESH)
    emb, rel_vec = n["emb"], n["rel_vec"]
    emb[...] = jnp.zeros_like(emb)
    rel_vec[...] = jnp.zeros_like(rel_vec)
    emb[:, :width] = n["emb_in"][...]
    n["accum_out"][...] = n["accum_in"][...]
    lane = iota((PER, 128), 1)

    def write_block(r):
        value = emb[...]
        block = n["block"].at[r]
        block[:, :TAIL] = value[:, :TAIL].astype(BF)
        block[:, TAIL:] = jnp.where(lane < width - TAIL, value[:, TAIL:], n["wanted"][r]).astype(BF)

    write_block(0)
    pl.semaphore_wait(barrier, len(everyone))

    def counts(row):
        neg = n["negatives"].shape[1]
        hot = (iota((touch, neg), 0) == n["negatives"][row : row + 1, :]).astype(BF)
        return mm(jnp.ones((8, neg), BF), hot, 1, 1)[:1] * (1.0 / neg)

    def prepare(r):
        if r == 0:
            table_copy.wait()
        hot = (iota((nrel, edges), 0) == n["rel_ids"][r : r + 1, :]).astype(BF)
        rel_vec[r, :, :width] = mm(hot, n["rel_table"][...], 0, 0)
        for side in range(2):
            n["count"][2 * r + side : 2 * r + side + 1, :] = counts(2 * r + side)

    def edge_step(r):
        own, far = n["own"][r], n["far"][r]
        head_hot = (iota((touch, edges), 0) == n["edge_slots"][2 * r : 2 * r + 1, :]).astype(BF)
        tail_hot = (iota((touch, edges), 0) == n["edge_slots"][2 * r + 1 : 2 * r + 2, :]).astype(BF)
        rel = rel_vec[r]
        head_vec = mm(head_hot, own, 0, 0)
        tail_vec = mm(tail_hot, far, 0, 0)
        positive = jnp.sum(head_vec * rel * tail_vec, axis=-1, keepdims=True)
        query_tail = (head_vec * rel).astype(BF)
        query_head = (tail_vec * rel).astype(BF)
        own_count = n["count"][2 * r : 2 * r + 1, :]
        far_count = n["count"][2 * r + 1 : 2 * r + 2, :]
        weight_tail = (jax.nn.sigmoid(mm(query_tail, far, 1, 1)) * far_count).astype(BF)
        weight_head = (jax.nn.sigmoid(mm(query_head, own, 1, 1)) * own_count).astype(BF)
        back_tail = mm(weight_tail, far, 1, 0)
        back_head = mm(weight_head, own, 1, 0)
        coeff = -jax.nn.sigmoid(-positive)

        def spread(hot, grad, weight, query):
            hi = grad.astype(BF)
            lo = (grad - hi.astype(F32)).astype(BF)
            return (mm(hot, hi, 1, 0) + mm(hot, lo, 1, 0) + mm(weight, query, 0, 0)).astype(BF)

        n["own_grad"][r] = spread(head_hot, rel * (coeff * tail_vec + back_tail), weight_head, query_head)
        n["far_grad"][r] = spread(tail_hot, rel * (coeff * head_vec + back_head), weight_tail, query_tail)
        grad_rel = coeff * head_vec * tail_vec + head_vec * back_tail + tail_vec * back_head
        rows = n["rows"].at[r, 0, pl.ds(0, edges)]
        rows[:, :TAIL] = grad_rel[:, :TAIL].astype(BF)
        rows[:, TAIL:] = jnp.where(iota((edges, 128), 1) < width - TAIL, grad_rel[:, TAIL:], n["rel_marks"][r]).astype(BF)

    def update(row_grad):
        accum = n["accum_out"][...] + jnp.sum(row_grad * row_grad, axis=-1, keepdims=True) * (1.0 / width)
        n["accum_out"][...] = accum
        emb[...] = emb[...] - LEARN_RATE * row_grad / jnp.sqrt(accum)

    def slot_rows(r, near, d):
        return n["rows"].at[r, near, pl.ds(d * edges, edges)]

    def x_copy(r, e):
        return remote(slot_rows(r, 0, 0), slot_rows(r, 0, e), n["x_send"].at[r, e], n["x_recv"].at[r, e], place.along_x(xs - e))

    def core_copy(r, d):
        return remote(slot_rows(r, 0, d), slot_rows(r, 1, d), n["core_send"].at[r, d], n["core_recv"].at[r, d], (place.mate, place.s))

    def rows_start(r):
        for e in range(1, xs):
            x_copy(r, e).start()
        core_copy(r, 0).start()

    def rows_forward(r):
        for e in range(1, xs):
            x_copy(r, e).wait_recv()
            core_copy(r, e).start()

    def rows_sum(r):
        for d in range(xs):
            core_copy(r, d).wait_recv()
        base = (place.x * INNER + place.core) * (2 * seg)
        total = n["dense"][...] if r else jnp.zeros((4 * seg, WIDE), F32)
        for near in range(2):
            block = n["rows"][r, near]
            marks = block[:, TAIL:].astype(F32)
            at = iota(marks.shape, 1)
            ids = jnp.sum(jnp.where(at == MARK, marks * 64.0, jnp.where(at == MARK + 1, marks, 0.0)), axis=1, keepdims=True)
            col = iota((xs * edges, 4 * seg), 1)
            target = base + col + jnp.where(col >= 2 * seg, 2 * seg, 0)
            total = total + mm((ids.astype(I32) == target).astype(BF), block, 0, 0)
        n["dense"][...] = total
        for e in range(1, xs):
            x_copy(r, e).wait_send()
        for d in range(xs):
            core_copy(r, d).wait_send()

    def seg_rows(ylo, yh):
        return pl.ds(pl.multiple_of((ylo * 2 + yh) * seg, seg), seg)

    def y_copy(k):
        ylo = place.ylo if k == 0 else 1 - place.ylo
        yh = place.yh if k == 1 else 1 - place.yh
        return remote(n["y_out"].at[seg_rows(ylo, yh)], n["y_in"].at[k], n["y_send"].at[k], n["y_recv"].at[k], place.peers(1)[k])

    def y_start():
        n["y_out"][...] = n["dense"][...].astype(BF)
        for k in range(3):
            y_copy(k).start()

    def z_copy(e):
        src = n["z_out"].at[lax.rem(place.z + zs - e, zs)]
        return remote(src, n["z_in"].at[e], n["z_send"].at[e], n["z_recv"].at[e], place.along_z(zs - e))

    def z_start():
        total = n["dense"][seg_rows(place.ylo, place.yh), :]
        for k in range(3):
            y_copy(k).wait_recv()
            total = total + n["y_in"][k].astype(F32)
        total = total.astype(BF)
        row, col = iota((zs * 16, seg), 0), iota((zs * 16, seg), 1)
        zz, k = row >> 4, row & 15
        packed = jnp.zeros((zs * 16, 128), F32)
        full = TAIL // 128
        for c in range(full):
            j = k - c * RELS
            hot = ((col == zz * RELS + j) & (j >= 0) & (j < RELS)).astype(BF)
            packed = packed + mm(hot, total[:, c * 128 : (c + 1) * 128], 1, 0)
        rest = width - TAIL
        last = total[:, TAIL:].astype(F32)
        last = jnp.where(iota(last.shape, 1) < rest, last, 0.0)
        for j in range(RELS):
            hot = ((col == zz * RELS + j) & (k == full * RELS)).astype(BF)
            moved = last if j == 0 else pltpu.roll(last, j * rest, 1)
            packed = packed + mm(hot, moved.astype(BF), 1, 0)
        packed = packed.astype(BF)
        for zz in range(zs):
            n["z_out"][zz] = packed[zz * 16 : (zz + 1) * 16]
        for e in range(1, zs):
            z_copy(e).start()

    def z_end():
        total = n["z_out"][place.z].astype(F32)
        for e in range(1, zs):
            z_copy(e).wait_recv()
            total = total + n["z_in"][e].astype(F32)
        n["rel_out"][...] = total
        for k in range(3):
            y_copy(k).wait_send()
        for e in range(1, zs):
            z_copy(e).wait_send()

    last_step = zs // 2
    for r in range(2):
        if r:
            write_block(r)
        fetch(
            place, r, slot, n["block"].at[r], n["line"].at[r], n["picked"].at[r], n["own"].at[r], n["far"].at[r], n["idx"].at[r],
            Ring(place, n["f_send"].at[r], n["f_recv"].at[r]), n["fp_send"].at[r], n["fp_recv"].at[r], n["f_self"].at[r],
            functools.partial(prepare, r),
        )
        edge_step(r)
        steps = {0: [functools.partial(rows_start, r)]}
        plan = ((2, functools.partial(rows_forward, r)), (4, functools.partial(rows_sum, r)))
        if r:
            plan = plan + ((4, y_start), (6, z_start))
        for t, what in plan:
            steps.setdefault(min(t, last_step), []).append(what)
        aside = {t: (lambda todo=todo: [f() for f in todo]) for t, todo in steps.items()}
        row_grad = give_back(
            place, r, slot, n["own_grad"].at[r], n["far_grad"].at[r], n["idx"].at[r], n["got"].at[r], n["term"], n["sent"].at[r], n["came"].at[r],
            Ring(place, n["s_send"].at[r], n["s_recv"].at[r]), n["sp_send"].at[r], n["sp_recv"].at[r], n["s_self"].at[r], aside,
        )
        update(row_grad)
    n["emb_out"][...] = emb[:, :width]
    z_end()


def run(emb, accum, relations, wanted, edge_slots, rel_ids, negatives, rel_marks, zs, xs, slot):
    width = emb.shape[1]
    touch = 2 * zs * slot
    edges = edge_slots.shape[1]
    half = zs // 2
    seg = zs * RELS
    dma = pltpu.SemaphoreType.DMA
    vmem = pltpu.VMEM
    inputs = dict(
        emb_in=emb, accum_in=accum, relations=relations, wanted=wanted, edge_slots=edge_slots, rel_ids=rel_ids,
        negatives=negatives, rel_marks=rel_marks,
    )
    outputs = dict(
        emb_out=jax.ShapeDtypeStruct(emb.shape, F32),
        accum_out=jax.ShapeDtypeStruct(accum.shape, F32),
        rel_out=jax.ShapeDtypeStruct((16, 128), F32),
    )
    scratch = dict(
        emb=vmem((PER, WIDE), F32),
        rel_table=vmem(relations.shape, BF),
        rel_vec=vmem((2, edges, WIDE), F32),
        count=vmem((4, touch), F32),
        block=vmem((2, PER, WIDE), BF),
        line=vmem((2, zs, PER, WIDE), BF),
        picked=vmem((2, zs, PER, WIDE), BF),
        own=vmem((2, touch, WIDE), BF),
        far=vmem((2, touch, WIDE), BF),
        idx=vmem((2, zs, 128), F32),
        own_grad=vmem((2, touch, WIDE), BF),
        far_grad=vmem((2, touch, WIDE), BF),
        got=vmem((2, zs, PER, WIDE), BF),
        term=vmem((zs, PER, WIDE), F32),
        sent=vmem((2, 2, half, 2, HALF, WIDE), BF),
        came=vmem((2, 2, half, 2, HALF, WIDE), BF),
        rows=vmem((2, 2, xs * edges, WIDE), BF),
        dense=vmem((4 * seg, WIDE), F32),
        y_out=vmem((4 * seg, WIDE), BF),
        y_in=vmem((3, seg, WIDE), BF),
        z_out=vmem((zs, 16, 128), BF),
        z_in=vmem((zs, 16, 128), BF),
        table_sem=dma,
        f_send=dma((2, 2, half, 2)),
        f_recv=dma((2, 2, half, 2)),
        fp_send=dma((2, 3)),
        fp_recv=dma((2, 3)),
        f_self=dma((2,)),
        s_send=dma((2, 2, half, 2)),
        s_recv=dma((2, 2, half, 2)),
        sp_send=dma((2, 3)),
        sp_recv=dma((2, zs, 3)),
        s_self=dma((2, zs)),
        x_send=dma((2, xs)),
        x_recv=dma((2, xs)),
        core_send=dma((2, xs)),
        core_recv=dma((2, xs)),
        y_send=dma((3,)),
        y_recv=dma((3,)),
        z_send=dma((zs,)),
        z_recv=dma((zs,)),
    )
    in_vmem = pl.BlockSpec(memory_space=pltpu.VMEM)
    names = (*inputs, *outputs, *scratch)
    return pl.pallas_call(
        functools.partial(main_kernel, zs, xs, slot, width, names),
        name="train_step",
        out_shape=tuple(outputs.values()),
        in_specs=[pl.BlockSpec(memory_space=pl.ANY) if k == "relations" else in_vmem for k in inputs],
        out_specs=(in_vmem,) * len(outputs),
        scratch_shapes=list(scratch.values()),
        compiler_params=pltpu.CompilerParams(collective_id=0, has_side_effects=True),
    )(*inputs.values())


def body(embeddings, row_accum, relations, relation_accum, request_rows, head_slots, tail_slots, relation_ids, own_negatives, far_negatives):
    rows, width = embeddings.shape
    slot = request_rows.shape[-1]
    zs = lax.axis_size("shard") // 2
    xs = lax.axis_size("dom") // INNER
    rounds, edges = head_slots.shape
    wanted = request_rows.reshape(rounds, 2, zs, 2 * slot).transpose(0, 2, 1, 3).reshape(rounds, zs, 4 * slot)
    wanted = jnp.pad(wanted, ((0, 0), (0, rows - zs), (MARK, 0))).astype(F32)
    marks = jnp.stack([relation_ids >> 6, relation_ids & 63], axis=-1)
    marks = jnp.pad(marks, ((0, 0), (0, 0), (MARK, 128 - MARK - 2))).astype(F32)
    edge_slots = jnp.stack([head_slots, tail_slots], axis=1).reshape(2 * rounds, edges)
    negatives = jnp.stack([own_negatives, far_negatives], axis=1).reshape(2 * rounds, -1)
    emb, accum, packed = run(
        embeddings, row_accum[:, None], relations, wanted, edge_slots, relation_ids, negatives, marks, zs, xs, slot
    )
    full, rest = width // 128, width % 128
    share = packed[: full * RELS].reshape(full, RELS, 128).transpose(1, 0, 2).reshape(RELS, full * 128)
    share = jnp.concatenate([share, packed[full * RELS, : RELS * rest].reshape(RELS, rest)], axis=1)
    new_relation_accum = relation_accum + jnp.mean(share * share, axis=-1)
    relation_step = -LEARN_RATE * share / jnp.sqrt(new_relation_accum)[:, None]
    return (emb, accum[:, 0], relation_step, new_relation_accum)


def solution(mesh):
    both = ("dom", "shard")
    return jax.shard_map(
        body,
        mesh=mesh,
        in_specs=(P(both, None), P(both), P(), P(both), P(None, both, None, None)) + (P(None, both),) * 5,
        out_specs=(P(both, None), P(both), P(both, None), P(both)),
        check_vma=False,
    )
```

time: 353 us -> 169 us (0.48)
  waiting for transfers between devices: 225 us -> 0 us
  Pallas kernels: 0 us -> 151 us
  starting transfers between devices: 62.1 us -> 0 us
  blocking collectives: 15.7 us -> 0 us
  matrix products: 14.3 us -> 0 us
  between operations: 14.6 us -> 0.69 us
    all_to_all x5 -> x0, waiting for transfers between devices: 199 us -> none  [the longest x2 99.6 us: body(): lax.all_to_all(served, 'shard', split_axis=0, concat_axis=0, tiled=True)]
    pallas_call x0 -> x1, Pallas kernels: none -> 151 us  [run(): pl.pallas_call(functools.partial(main_kernel, zs, xs, slot, width, names)...]
    all_to_all x5 -> x0, starting transfers between devices: 52.7 us -> none  [the longest x2 26.4 us: body(): lax.all_to_all(served, 'shard', split_axis=0, concat_axis=0, tiled=True)]
    ppermute x4 -> x0, waiting for transfers between devices: 20.5 us -> none  [partner(): return lax.ppermute(value, axis, pairs)]
    all_gather x1 -> x0, blocking collectives: 15.7 us -> none  [body(): ids = lax.all_gather(relation_ids.reshape(-1), 'dom', tiled=True)]
    dot_general x29 -> x0, matrix products: 14.3 us -> none  [mm(): lax.dot_general(a, b, (((ca,), (cb,)), ((), ())), preferred_element_type=...]
    ppermute x4 -> x0, starting transfers between devices: 9.33 us -> none  [partner(): return lax.ppermute(value, axis, pairs)]
    all_gather x1 -> x0, waiting for transfers between devices: 5.08 us -> none  [body(): group_rows = lax.all_gather(mine, 'dom', tiled=True)]
  transfers between devices with their start and end apart: 10 -> 0, of which waited for: 10 -> 0; matrix products, arithmetic and copies ran while one was open for 5% -> 0% of each run, Pallas kernels for 0% -> 0%
where the time goes in v3:
time: 169 us
  Pallas kernels  151 us (89%)
  local copies, waits for them, and re-layouts  11.2 us (7%)
  other arithmetic  6.34 us (4%)
    pallas_call x1, Pallas kernels, run(): pl.pallas_call(functools.partial(main_kernel, zs, xs, slot, width, names)...  151 us
    unnamed x4, local copies, waits for them, and re-layouts  5.84 us

profile of v3, /device:TPU:6, one launch (start us, length us, event | category | flops | bytes accessed | tf_op | source)
XLA Modules:
  0.0 168.8 jit_solution(597655500977210568)
XLA Ops:
  0.6 0.7 pad_add_fusion.2
  1.3 0.6 copy.38
  1.9 0.7 shift-right-arithmetic_bitcast_fusion
  2.6 0.7 pad_add_fusion.1
  3.3 0.6 reshape.30.refs_6_
  3.9 1.4 copy.42.refs_1_
  5.3 0.9 reshape.33
  6.2 0.1 copy.44
  6.3 0.1 reshape.28
  6.3 0.7 pad_convert_fusion.1.refs_3_
  7.0 0.1 copy.40
  7.2 0.1 copy.41
  7.3 0.1 pad_add_fusion
  7.4 0.8 pad_convert_fusion.refs_7_
  8.2 4.3 %copy.43.refs_2_ = bf16[2560,400]{1,0:T(8,128)(2,1)} copy(bf16[2560,400]{0,1:T(8,128)(2,1)} %param.12) | data formatting | bytes 4096000 | tf_op args[2]
  12.5 0.0 copy-start
  12.5 150.6 %train_step.1 = (f32[64,400]{1,0:T(8,128)}, f32[64,1]{1,0:T(8,128)}, f32[16,128]{1,0:T(8,128)}) custom-call(f32[64,400]{1,0:T(8,128)} %refs_0_.1, f32[64,1]{1,0:T(8,128)} %copy.42.refs_1_, bf16[2560,400]{1,0:T(8,128)(2,1)} %copy.43.refs_2_, f32[2,64,128]{2,1,0:T(8,128)} %pad_convert_fusion.1.refs_3_, s32[4,128]{1,0:T(4,128)} %bitcast.22, s32[2,128]{1,0:T(2,128)} %refs_5_.1, ...), custom_call_target="tpu_custom_call" | custom-call | tf_op jit(solution)/shard_map/train_step/pallas_call | solution.py:474
  163.0 1.4 reduce
  164.4 0.7 slice_reduce_fusion
  165.1 0.1 reshape_squeeze.3
  165.2 0.7 reshape.31
  165.9 0.1 multiply_reduce_fusion
  166.0 0.0 copy-done
  166.0 0.5 fusion
  166.6 0.7 multiply_divide_fusion
  167.2 1.6 copy.46
  (2 shorter events, 0.0 us)
Async XLA Ops:
  12.5 153.6 %copy-start = (f32[5]{0:T(128)S(1)}, f32[5]{0:T(128)}, u32[]{:S(2)}) copy-start(f32[5]{0:T(128)} %param.13) | copy-start | bytes 64

commit v4 on v3

--- a/solution.py
+++ b/solution.py
@@ -31,6 +31,16 @@
 
 def hops(zs):
     return ((zs // 2, zs - 1 - zs // 2), (zs - 1 - zs // 2, zs // 2))
+
+
+def column(row, rows):
+    n = row.shape[1]
+    return jnp.sum(jnp.where(iota((rows, n), 0) == iota((rows, n), 1), row, jnp.zeros_like(row)), axis=1, keepdims=True)
+
+
+def as_row(col, n):
+    rows = col.shape[0]
+    return jnp.sum(jnp.where(iota((rows, n), 0) == iota((rows, n), 1), col, jnp.zeros_like(col)), axis=0, keepdims=True)
 
 
 def remote(src, dst, send, recv, device):
@@ -82,11 +92,19 @@
     def __init__(self, place, send, recv):
         self.place, self.send, self.recv = place, send, recv
         self.count = hops(place.zs)
-
-    def copy(self, src, dst, direction, t, c):
+        self.far = place.zs // 2
+        self.jump = place.zs // 4 + 1
+        near, rest = list(range(1, self.jump)), list(range(self.jump, self.far + 1))
+        self.order = []
+        while near or rest:
+            for lane in (near, rest):
+                if lane:
+                    self.order.append(lane.pop(0))
+
+    def copy(self, src, dst, direction, t, c, hop):
         return remote(
             src, dst, self.send.at[direction, t - 1, c], self.recv.at[direction, t - 1, c],
-            self.place.along_z(1 if direction == 0 else self.place.zs - 1),
+            self.place.along_z(hop if direction == 0 else self.place.zs - hop),
         )
 
     def each(self, t):
@@ -100,13 +118,14 @@
     return ref.at[pl.ds(c * HALF, HALF)]
 
 
-def fetch(place, r, slot, block, line, picked, own, far, idx, ring, peer_send, peer_recv, self_sem, prepare):
+def fetch(place, r, slot, block, line, picked, own, far, idx, ring, peer_send, peer_recv, self_sem):
     zs, peers = place.zs, place.peers(r)
 
     def step(direction, t, c):
         sign = -1 if direction == 0 else 1
-        src = piece(block, c) if t == 1 else piece(line.at[(sign * (t - 1)) % zs], c)
-        return ring.copy(src, piece(line.at[(sign * t) % zs], c), direction, t, c)
+        first = t in (1, ring.jump)
+        src = piece(block, c) if first else piece(line.at[(sign * (t - 1)) % zs], c)
+        return ring.copy(src, piece(line.at[(sign * t) % zs], c), direction, t, c, t if first else 1)
 
     def select(d):
         value = block[...] if d == 0 else line[d]
@@ -122,14 +141,14 @@
         for k, (start, dst) in enumerate(((theirs, own), (mine + slot, far), (theirs + slot, far))):
             remote(picked.at[d, pl.ds(start, slot)], dst.at[at], peer_send.at[k], peer_recv.at[k], peers[k]).start()
 
-    for direction, c in ring.each(1):
-        step(direction, 1, c).start()
+    for t in dict.fromkeys((ring.jump, 1)):
+        for direction, c in ring.each(t):
+            step(direction, t, c).start()
     select(0)
-    prepare()
-    for t in range(1, zs // 2 + 1):
+    for t in ring.order:
         for direction, c in ring.each(t):
             step(direction, t, c).wait_recv()
-            if t + 1 <= ring.count[c][direction]:
+            if t + 1 <= ring.count[c][direction] and t + 1 != ring.jump:
                 step(direction, t + 1, c).start()
         select(zs - t)
         if t != zs // 2:
@@ -159,8 +178,9 @@
             remote(far.at[there], k1, peer_send.at[2], peer_recv.at[d, 2], peers[2]),
         )
 
-    def step(direction, t, c):
-        return ring.copy(sent.at[direction, t - 1, c], came.at[direction, t - 1, c], direction, t, c)
+    def step(direction, d, c):
+        hop = d if d == ring.jump else 1
+        return ring.copy(sent.at[direction, d - 1, c], came.at[direction, d - 1, c], direction, d, c, hop)
 
     def make_term(d):
         copies = exchange(d)
@@ -170,38 +190,39 @@
         hot = (iota((PER, PER), 0) == idx[d : d + 1, MARK:].astype(I32)).astype(BF)
         term[d] = mm(hot, got[d], 1, 0)
 
-    for t in range(zs // 2, 0, -1):
-        for d in (t,) if t == zs // 2 else (t, zs - t):
+    order = ring.order[::-1]
+    order = sorted(order, key=lambda t: (ring.far - t) if t >= ring.jump else (ring.jump - 1 - t) + 1.5)
+    for t in order:
+        for d in (t,) if t == ring.far else (t, zs - t):
             for copy in exchange(d):
                 copy.start()
     for copy in exchange(0):
         copy.start()
     aside[0]()
     made = set()
-    for t in range(1, zs // 2 + 1):
+    for number, t in enumerate(order):
         for direction, c in ring.each(t):
-            d = ring.count[c][direction] - t + 1
-            d = d % zs if direction == 0 else (-d) % zs
+            d = t if direction == 0 else zs - t
             if d not in made:
                 make_term(d)
                 made.add(d)
             value = term[d, pl.ds(c * HALF, HALF)]
-            if t > 1:
-                step(direction, t - 1, c).wait_recv()
-                value = value + came[direction, t - 2, c].astype(F32)
+            if t < ring.count[c][direction] and t + 1 != ring.jump:
+                step(direction, t + 1, c).wait_recv()
+                value = value + came[direction, t, c].astype(F32)
             sent[direction, t - 1, c] = value.astype(BF)
             step(direction, t, c).start()
-        if t in aside:
-            aside[t]()
+        if number + 1 in aside:
+            aside[number + 1]()
     make_term(0)
     halves = []
     for c in range(2):
         value = term[0, pl.ds(c * HALF, HALF)]
         for direction in range(2):
-            count = ring.count[c][direction]
-            if count:
-                step(direction, count, c).wait_recv()
-                value = value + came[direction, count - 1, c].astype(F32)
+            for t in dict.fromkeys((1, ring.jump)):
+                if t <= ring.count[c][direction]:
+                    step(direction, t, c).wait_recv()
+                    value = value + came[direction, t - 1, c].astype(F32)
         halves.append(value)
     for t in range(1, zs // 2 + 1):
         for direction, c in ring.each(t):
@@ -216,8 +237,8 @@
     n = dict(zip(names, refs))
     place = Place(zs, xs)
     touch = 2 * zs * slot
-    edges = n["edge_slots"].shape[1]
-    nrel = n["rel_table"].shape[0]
+    edges = n["heads"].shape[1]
+    nrel = n["rel_table"].shape[1]
     seg = zs * RELS
 
     table_copy = pltpu.make_async_copy(n["relations"], n["rel_table"], n["table_sem"])
@@ -230,35 +251,47 @@
     emb[...] = jnp.zeros_like(emb)
     rel_vec[...] = jnp.zeros_like(rel_vec)
     emb[:, :width] = n["emb_in"][...]
-    n["accum_out"][...] = n["accum_in"][...]
+    n["accum"][...] = column(n["accum_in"][...], PER)
     lane = iota((PER, 128), 1)
 
     def write_block(r):
         value = emb[...]
         block = n["block"].at[r]
         block[:, :TAIL] = value[:, :TAIL].astype(BF)
-        block[:, TAIL:] = jnp.where(lane < width - TAIL, value[:, TAIL:], n["wanted"][r]).astype(BF)
+        block[:, TAIL:] = jnp.where(lane < width - TAIL, value[:, TAIL:], 0.0).astype(BF)
+        requests = n["requests"][r].astype(BF)
+        kj, q = requests.shape
+        wanted = jnp.zeros((16, 128), F32)
+        for yh in range(2):
+            mine = iota((16, q), 0)
+            pick = ((iota((16, q), 1) == mine + yh * zs) & (mine < zs)).astype(BF)
+            put = (iota((kj, 128), 1) == iota((kj, 128), 0) + (MARK + yh * kj)).astype(BF)
+            wanted = wanted + mm(mm(pick, requests, 1, 1).astype(BF), put, 1, 0)
+        block[:16, TAIL:] = jnp.where(lane[:16] < width - TAIL, value[:16, TAIL:], wanted).astype(BF)
 
     write_block(0)
+
+    def counts(ids):
+        neg = ids.shape[1]
+        hot = (iota((touch, neg), 0) == ids).astype(BF)
+        return mm(jnp.ones((8, neg), BF), hot, 1, 1)[:1] * (1.0 / neg)
+
+    def rel_column(r):
+        return column(n["rel_ids"][r : r + 1, :], edges)
+
+    for r in range(2):
+        for side, name in enumerate(("own_neg", "far_neg")):
+            n["count"][2 * r + side : 2 * r + side + 1, :] = counts(n[name][r : r + 1, :])
+    table_copy.wait()
+    for r in range(2):
+        hot = (iota((edges, nrel), 1) == rel_column(r)).astype(BF)
+        rel_vec[r, :, :width] = mm(hot, n["rel_table"][...], 1, 1)
     pl.semaphore_wait(barrier, len(everyone))
-
-    def counts(row):
-        neg = n["negatives"].shape[1]
-        hot = (iota((touch, neg), 0) == n["negatives"][row : row + 1, :]).astype(BF)
-        return mm(jnp.ones((8, neg), BF), hot, 1, 1)[:1] * (1.0 / neg)
-
-    def prepare(r):
-        if r == 0:
-            table_copy.wait()
-        hot = (iota((nrel, edges), 0) == n["rel_ids"][r : r + 1, :]).astype(BF)
-        rel_vec[r, :, :width] = mm(hot, n["rel_table"][...], 0, 0)
-        for side in range(2):
-            n["count"][2 * r + side : 2 * r + side + 1, :] = counts(2 * r + side)
 
     def edge_step(r):
         own, far = n["own"][r], n["far"][r]
-        head_hot = (iota((touch, edges), 0) == n["edge_slots"][2 * r : 2 * r + 1, :]).astype(BF)
-        tail_hot = (iota((touch, edges), 0) == n["edge_slots"][2 * r + 1 : 2 * r + 2, :]).astype(BF)
+        head_hot = (iota((touch, edges), 0) == n["heads"][r : r + 1, :]).astype(BF)
+        tail_hot = (iota((touch, edges), 0) == n["tails"][r : r + 1, :]).astype(BF)
         rel = rel_vec[r]
         head_vec = mm(head_hot, own, 0, 0)
         tail_vec = mm(tail_hot, far, 0, 0)
@@ -283,11 +316,13 @@
         grad_rel = coeff * head_vec * tail_vec + head_vec * back_tail + tail_vec * back_head
         rows = n["rows"].at[r, 0, pl.ds(0, edges)]
         rows[:, :TAIL] = grad_rel[:, :TAIL].astype(BF)
-        rows[:, TAIL:] = jnp.where(iota((edges, 128), 1) < width - TAIL, grad_rel[:, TAIL:], n["rel_marks"][r]).astype(BF)
+        at, ids = iota((edges, 128), 1), rel_column(r)
+        marks = jnp.where(at == MARK, ids >> 6, jnp.where(at == MARK + 1, ids & 63, 0)).astype(F32)
+        rows[:, TAIL:] = jnp.where(at < width - TAIL, grad_rel[:, TAIL:], marks).astype(BF)
 
     def update(row_grad):
-        accum = n["accum_out"][...] + jnp.sum(row_grad * row_grad, axis=-1, keepdims=True) * (1.0 / width)
-        n["accum_out"][...] = accum
+        accum = n["accum"][...] + jnp.sum(row_grad * row_grad, axis=-1, keepdims=True) * (1.0 / width)
+        n["accum"][...] = accum
         emb[...] = emb[...] - LEARN_RATE * row_grad / jnp.sqrt(accum)
 
     def slot_rows(r, near, d):
@@ -377,7 +412,22 @@
         for e in range(1, zs):
             z_copy(e).wait_recv()
             total = total + n["z_in"][e].astype(F32)
-        n["rel_out"][...] = total
+        share = n["share"]
+        share[...] = jnp.zeros_like(share)
+        full, rest = TAIL // 128, width - TAIL
+        for c in range(full):
+            share[:RELS, c * 128 : (c + 1) * 128] = total[c * RELS : (c + 1) * RELS, :]
+        for j in range(RELS):
+            last = total[full * RELS : full * RELS + 1, :]
+            last = last if j == 0 else pltpu.roll(last, 128 - j * rest, 1)
+            share[j : j + 1, TAIL:] = jnp.where(iota((1, 128), 1) < rest, last, 0.0)
+        value = share[...]
+        squares = jnp.sum(value * value, axis=-1, keepdims=True) * (1.0 / width)
+        rel_accum = column(n["rel_accum"][...], value.shape[0]) + squares
+        rel_accum = jnp.where(iota(rel_accum.shape, 0) < RELS, rel_accum, 1.0)
+        value = -LEARN_RATE * value / jnp.sqrt(rel_accum)
+        n["step_out"][...] = value[:RELS, :width]
+        n["rel_accum_out"][...] = as_row(rel_accum, RELS)
         for k in range(3):
             y_copy(k).wait_send()
         for e in range(1, zs):
@@ -390,7 +440,6 @@
         fetch(
             place, r, slot, n["block"].at[r], n["line"].at[r], n["picked"].at[r], n["own"].at[r], n["far"].at[r], n["idx"].at[r],
             Ring(place, n["f_send"].at[r], n["f_recv"].at[r]), n["fp_send"].at[r], n["fp_recv"].at[r], n["f_self"].at[r],
-            functools.partial(prepare, r),
         )
         edge_step(r)
         steps = {0: [functools.partial(rows_start, r)]}
@@ -406,29 +455,29 @@
         )
         update(row_grad)
     n["emb_out"][...] = emb[:, :width]
+    n["accum_out"][...] = as_row(n["accum"][...], PER)
     z_end()
 
 
-def run(emb, accum, relations, wanted, edge_slots, rel_ids, negatives, rel_marks, zs, xs, slot):
-    width = emb.shape[1]
+def run(inputs, zs, xs, slot):
+    width = inputs["emb_in"].shape[1]
     touch = 2 * zs * slot
-    edges = edge_slots.shape[1]
+    edges = inputs["heads"].shape[1]
     half = zs // 2
     seg = zs * RELS
     dma = pltpu.SemaphoreType.DMA
     vmem = pltpu.VMEM
-    inputs = dict(
-        emb_in=emb, accum_in=accum, relations=relations, wanted=wanted, edge_slots=edge_slots, rel_ids=rel_ids,
-        negatives=negatives, rel_marks=rel_marks,
-    )
     outputs = dict(
-        emb_out=jax.ShapeDtypeStruct(emb.shape, F32),
-        accum_out=jax.ShapeDtypeStruct(accum.shape, F32),
-        rel_out=jax.ShapeDtypeStruct((16, 128), F32),
+        emb_out=jax.ShapeDtypeStruct((PER, width), F32),
+        accum_out=jax.ShapeDtypeStruct((1, PER), F32),
+        step_out=jax.ShapeDtypeStruct((RELS, width), F32),
+        rel_accum_out=jax.ShapeDtypeStruct((1, RELS), F32),
     )
     scratch = dict(
         emb=vmem((PER, WIDE), F32),
-        rel_table=vmem(relations.shape, BF),
+        rel_table=vmem(inputs["relations"].shape, BF),
+        accum=vmem((PER, 1), F32),
+        share=vmem((8, WIDE), F32),
         rel_vec=vmem((2, edges, WIDE), F32),
         count=vmem((4, touch), F32),
         block=vmem((2, PER, WIDE), BF),
@@ -483,26 +532,21 @@
 
 
 def body(embeddings, row_accum, relations, relation_accum, request_rows, head_slots, tail_slots, relation_ids, own_negatives, far_negatives):
-    rows, width = embeddings.shape
-    slot = request_rows.shape[-1]
-    zs = lax.axis_size("shard") // 2
-    xs = lax.axis_size("dom") // INNER
-    rounds, edges = head_slots.shape
-    wanted = request_rows.reshape(rounds, 2, zs, 2 * slot).transpose(0, 2, 1, 3).reshape(rounds, zs, 4 * slot)
-    wanted = jnp.pad(wanted, ((0, 0), (0, rows - zs), (MARK, 0))).astype(F32)
-    marks = jnp.stack([relation_ids >> 6, relation_ids & 63], axis=-1)
-    marks = jnp.pad(marks, ((0, 0), (0, 0), (MARK, 128 - MARK - 2))).astype(F32)
-    edge_slots = jnp.stack([head_slots, tail_slots], axis=1).reshape(2 * rounds, edges)
-    negatives = jnp.stack([own_negatives, far_negatives], axis=1).reshape(2 * rounds, -1)
-    emb, accum, packed = run(
-        embeddings, row_accum[:, None], relations, wanted, edge_slots, relation_ids, negatives, marks, zs, xs, slot
+    rounds, shards, sides, slot = request_rows.shape
+    inputs = dict(
+        emb_in=embeddings,
+        accum_in=row_accum[None, :],
+        relations=relations.T,
+        rel_accum=relation_accum[None, :],
+        requests=request_rows.transpose(0, 2, 3, 1).reshape(rounds, sides * slot, shards),
+        heads=head_slots,
+        tails=tail_slots,
+        rel_ids=relation_ids,
+        own_neg=own_negatives,
+        far_neg=far_negatives,
     )
-    full, rest = width // 128, width % 128
-    share = packed[: full * RELS].reshape(full, RELS, 128).transpose(1, 0, 2).reshape(RELS, full * 128)
-    share = jnp.concatenate([share, packed[full * RELS, : RELS * rest].reshape(RELS, rest)], axis=1)
-    new_relation_accum = relation_accum + jnp.mean(share * share, axis=-1)
-    relation_step = -LEARN_RATE * share / jnp.sqrt(new_relation_accum)[:, None]
-    return (emb, accum[:, 0], relation_step, new_relation_accum)
+    emb, accum, step, rel_accum = run(inputs, shards // 2, lax.axis_size("dom") // INNER, slot)
+    return (emb, accum[0], step, rel_accum[0])
 
 
 def solution(mesh):

time: 169 us -> 141 us (0.83)
  Pallas kernels: 151 us -> 134 us
  other arithmetic: 6.34 us -> 0 us
  local copies, waits for them, and re-layouts: 11.2 us -> 5.19 us
    pallas_call x1, Pallas kernels: 151 us -> 134 us  [run(): pl.pallas_call(functools.partial(main_kernel, zs, xs, slot, width, names)...]
    reshape x5 -> x0, local copies, waits for them, and re-layouts: 2.33 us -> none  [the longest x3 1.02 us: body(): request_rows.reshape(rounds, 2, zs, 2 * slot).transpose(0, 2, 1, 3)]
    another operation x4 -> x0, other arithmetic: 2.19 us -> none  [the longest x2 0.79 us: body(): marks = jnp.stack([relation_ids >> 6, relation_ids & 63], axis=-1)]
where the time goes in v4:
time: 141 us; the launch traced here: 140 us
  Pallas kernels  134 us (95%)
  local copies, waits for them, and re-layouts  5.19 us (4%)
    pallas_call x1, Pallas kernels, run(): pl.pallas_call(functools.partial(main_kernel, zs, xs, slot, width, names)...  134 us
    unnamed x4, local copies, waits for them, and re-layouts  5.19 us

profile of v4, /device:TPU:6, one launch (start us, length us, event | category | flops | bytes accessed | tf_op | source)
XLA Modules:
  0.0 140.2 jit_solution(9509625923990519)
XLA Ops:
  0.6 134.3 %train_step.1 = (f32[64,400]{1,0:T(8,128)}, f32[1,64]{1,0:T(1,128)}, f32[5,400]{1,0:T(8,128)}, f32[1,5]{1,0:T(1,128)}) custom-call(f32[64,400]{1,0:T(8,128)} %refs_0_.1, f32[1,64]{1,0:T(1,128)} %bitcast.10, bf16[400,2560]{1,0:T(8,128)(2,1)} %bitcast.8, f32[1,5]{1,0:T(1,128)} %bitcast.11, s32[2,32,32]{2,1,0:T(8,128)} %bitcast.9, s32[2,128]{1,0:T(2,128)} %refs_5_.1, ...), custom_call_target="tpu_custom_call" | custom-call | tf_op jit(solution)/shard_map/train_step/pallas_call | solution.py:523
  135.0 1.6 %copy.18 = f32[64,400]{1,0:T(8,128)} copy(f32[64,400]{1,0:T(8,128)} %get-tuple-element.16) | data formatting | bytes 204800
  136.5 1.2 copy.19
  137.7 1.3 copy.20
  139.0 1.1 copy.21

commit v5 on v4

--- a/solution.py
+++ b/solution.py
@@ -16,7 +16,10 @@
 TAIL = WIDE - 128
 MARK = 64
 PER = 64
-HALF = PER // 2
+REST = 16
+FULL = 3 * PER
+PACKED = FULL + 16
+CUTS = ((0, 112), (112, PACKED))
 RELS = 5
 INNER = 4
 
@@ -115,10 +118,29 @@
 
 
 def piece(ref, c):
-    return ref.at[pl.ds(c * HALF, HALF)]
-
-
-def fetch(place, r, slot, block, line, picked, own, far, idx, ring, peer_send, peer_recv, self_sem):
+    return ref.at[pl.ds(CUTS[c][0], CUTS[c][1] - CUTS[c][0])]
+
+
+def fold(last):
+    keep = iota((8, 128), 1) < REST
+    total = jnp.zeros((8, 128), F32)
+    for m in range(8):
+        part = jnp.where(keep, last[m * 8 : (m + 1) * 8], 0.0)
+        total = total + (part if m == 0 else pltpu.roll(part, m * REST, 1))
+    return total
+
+
+def unfold(folded):
+    keep = iota((8, 128), 1) < REST
+    parts = [folded if m == 0 else pltpu.roll(folded, 128 - m * REST, 1) for m in range(8)]
+    return jnp.concatenate([jnp.where(keep, part, 0.0) for part in parts], axis=0)
+
+
+def widen(packed, last):
+    return jnp.concatenate([packed[c * PER : (c + 1) * PER] for c in range(3)] + [last], axis=1)
+
+
+def fetch(place, r, slot, block, line, picked, own, far, idx, ring, peer_send, peer_recv, self_sem, beside):
     zs, peers = place.zs, place.peers(r)
 
     def step(direction, t, c):
@@ -129,11 +151,13 @@
 
     def select(d):
         value = block[...] if d == 0 else line[d]
-        table = value[:16, TAIL:].astype(F32)
-        ids = jnp.sum(jnp.where(iota(table.shape, 0) == place.z, table, 0.0), axis=0, keepdims=True)
+        tail = value[FULL:].astype(F32)
+        table = tail[8:]
+        ids = jnp.sum(jnp.where(iota(table.shape, 0) == lax.rem(place.z, 8), table, 0.0), axis=0, keepdims=True)
+        ids = jnp.where(place.z >= 8, pltpu.roll(ids, 64, 1), ids)
         idx[d : d + 1, :] = ids
-        hot = (iota((PER, PER), 0) == ids[:, MARK:].astype(I32)).astype(BF)
-        picked[d] = mm(hot, value, 0, 0).astype(BF)
+        hot = (iota((PER, PER), 0) == ids[:, :PER].astype(I32)).astype(BF)
+        picked[d] = mm(hot, widen(value, unfold(tail[:8]).astype(BF)), 0, 0).astype(BF)
         at = place.owner_rows(place.yh, d, slot)
         mine = place.yh * 2 * slot
         theirs = (1 - place.yh) * 2 * slot
@@ -145,6 +169,7 @@
         for direction, c in ring.each(t):
             step(direction, t, c).start()
     select(0)
+    beside()
     for t in ring.order:
         for direction, c in ring.each(t):
             step(direction, t, c).wait_recv()
@@ -180,15 +205,18 @@
 
     def step(direction, d, c):
         hop = d if d == ring.jump else 1
-        return ring.copy(sent.at[direction, d - 1, c], came.at[direction, d - 1, c], direction, d, c, hop)
+        return ring.copy(piece(sent.at[direction, d - 1], c), piece(came.at[direction, d - 1], c), direction, d, c, hop)
 
     def make_term(d):
         copies = exchange(d)
         copies[0].wait()
         for copy in copies[1:]:
             copy.wait_recv()
-        hot = (iota((PER, PER), 0) == idx[d : d + 1, MARK:].astype(I32)).astype(BF)
-        term[d] = mm(hot, got[d], 1, 0)
+        hot = (iota((PER, PER), 0) == idx[d : d + 1, :PER].astype(I32)).astype(BF)
+        value = mm(hot, got[d], 1, 0)
+        for c in range(3):
+            term[d, c * PER : (c + 1) * PER] = value[:, c * 128 : (c + 1) * 128]
+        term[d, FULL:] = jnp.concatenate([fold(value[:, TAIL:]), jnp.zeros((8, 128), F32)], axis=0)
 
     order = ring.order[::-1]
     order = sorted(order, key=lambda t: (ring.far - t) if t >= ring.jump else (ring.jump - 1 - t) + 1.5)
@@ -206,23 +234,25 @@
             if d not in made:
                 make_term(d)
                 made.add(d)
-            value = term[d, pl.ds(c * HALF, HALF)]
+            low, high = CUTS[c]
+            value = term[d, low:high]
             if t < ring.count[c][direction] and t + 1 != ring.jump:
                 step(direction, t + 1, c).wait_recv()
-                value = value + came[direction, t, c].astype(F32)
-            sent[direction, t - 1, c] = value.astype(BF)
+                value = value + came[direction, t, low:high].astype(F32)
+            sent[direction, t - 1, low:high] = value.astype(BF)
             step(direction, t, c).start()
         if number + 1 in aside:
             aside[number + 1]()
     make_term(0)
     halves = []
     for c in range(2):
-        value = term[0, pl.ds(c * HALF, HALF)]
+        low, high = CUTS[c]
+        value = term[0, low:high]
         for direction in range(2):
             for t in dict.fromkeys((1, ring.jump)):
                 if t <= ring.count[c][direction]:
                     step(direction, t, c).wait_recv()
-                    value = value + came[direction, t - 1, c].astype(F32)
+                    value = value + came[direction, t - 1, low:high].astype(F32)
         halves.append(value)
     for t in range(1, zs // 2 + 1):
         for direction, c in ring.each(t):
@@ -230,7 +260,8 @@
     whole = own.at[pl.ds(0, zs * slot)]
     for k in range(3):
         remote(whole, whole, peer_send.at[k], peer_recv.at[0, k], peers[k]).wait_send()
-    return jnp.concatenate(halves, axis=0)
+    total = jnp.concatenate(halves, axis=0)
+    return widen(total, unfold(total[FULL : FULL + 8]))
 
 
 def main_kernel(zs, xs, slot, width, names, *refs):
@@ -252,22 +283,22 @@
     rel_vec[...] = jnp.zeros_like(rel_vec)
     emb[:, :width] = n["emb_in"][...]
     n["accum"][...] = column(n["accum_in"][...], PER)
-    lane = iota((PER, 128), 1)
 
     def write_block(r):
         value = emb[...]
         block = n["block"].at[r]
-        block[:, :TAIL] = value[:, :TAIL].astype(BF)
-        block[:, TAIL:] = jnp.where(lane < width - TAIL, value[:, TAIL:], 0.0).astype(BF)
+        for c in range(3):
+            block[c * PER : (c + 1) * PER] = value[:, c * 128 : (c + 1) * 128].astype(BF)
         requests = n["requests"][r].astype(BF)
         kj, q = requests.shape
-        wanted = jnp.zeros((16, 128), F32)
-        for yh in range(2):
-            mine = iota((16, q), 0)
-            pick = ((iota((16, q), 1) == mine + yh * zs) & (mine < zs)).astype(BF)
-            put = (iota((kj, 128), 1) == iota((kj, 128), 0) + (MARK + yh * kj)).astype(BF)
-            wanted = wanted + mm(mm(pick, requests, 1, 1).astype(BF), put, 1, 0)
-        block[:16, TAIL:] = jnp.where(lane[:16] < width - TAIL, value[:16, TAIL:], wanted).astype(BF)
+        wanted = jnp.zeros((8, 128), F32)
+        for part in range(2):
+            for yh in range(2):
+                at = iota((8, q), 0) + part * 8
+                pick = ((iota((8, q), 1) == at + yh * zs) & (at < zs)).astype(BF)
+                put = (iota((kj, 128), 1) == iota((kj, 128), 0) + (part * 64 + yh * kj)).astype(BF)
+                wanted = wanted + mm(mm(pick, requests, 1, 1).astype(BF), put, 1, 0)
+        block[FULL:] = jnp.concatenate([fold(value[:, TAIL:]), wanted], axis=0).astype(BF)
 
     write_block(0)
 
@@ -440,12 +471,13 @@
         fetch(
             place, r, slot, n["block"].at[r], n["line"].at[r], n["picked"].at[r], n["own"].at[r], n["far"].at[r], n["idx"].at[r],
             Ring(place, n["f_send"].at[r], n["f_recv"].at[r]), n["fp_send"].at[r], n["fp_recv"].at[r], n["f_self"].at[r],
+            functools.partial(rows_sum, 0) if r else (lambda: None),
         )
         edge_step(r)
         steps = {0: [functools.partial(rows_start, r)]}
-        plan = ((2, functools.partial(rows_forward, r)), (4, functools.partial(rows_sum, r)))
+        plan = ((2, functools.partial(rows_forward, r)),)
         if r:
-            plan = plan + ((4, y_start), (6, z_start))
+            plan = plan + ((4, functools.partial(rows_sum, r)), (4, y_start), (6, z_start))
         for t, what in plan:
             steps.setdefault(min(t, last_step), []).append(what)
         aside = {t: (lambda todo=todo: [f() for f in todo]) for t, todo in steps.items()}
@@ -480,8 +512,8 @@
         share=vmem((8, WIDE), F32),
         rel_vec=vmem((2, edges, WIDE), F32),
         count=vmem((4, touch), F32),
-        block=vmem((2, PER, WIDE), BF),
-        line=vmem((2, zs, PER, WIDE), BF),
+        block=vmem((2, PACKED, 128), BF),
+        line=vmem((2, zs, PACKED, 128), BF),
         picked=vmem((2, zs, PER, WIDE), BF),
         own=vmem((2, touch, WIDE), BF),
         far=vmem((2, touch, WIDE), BF),
@@ -489,9 +521,9 @@
         own_grad=vmem((2, touch, WIDE), BF),
         far_grad=vmem((2, touch, WIDE), BF),
         got=vmem((2, zs, PER, WIDE), BF),
-        term=vmem((zs, PER, WIDE), F32),
-        sent=vmem((2, 2, half, 2, HALF, WIDE), BF),
-        came=vmem((2, 2, half, 2, HALF, WIDE), BF),
+        term=vmem((zs, PACKED, 128), F32),
+        sent=vmem((2, 2, half, PACKED, 128), BF),
+        came=vmem((2, 2, half, PACKED, 128), BF),
         rows=vmem((2, 2, xs * edges, WIDE), BF),
         dense=vmem((4 * seg, WIDE), F32),
         y_out=vmem((4 * seg, WIDE), BF),
@@ -531,6 +563,23 @@
     )(*inputs.values())
 
 
+def finish_kernel(*refs):
+    half = len(refs) // 2
+    for src, dst in zip(refs[:half], refs[half:]):
+        dst[...] = src[...]
+
+
+def finish(*values):
+    in_vmem = pl.BlockSpec(memory_space=pltpu.VMEM)
+    return pl.pallas_call(
+        finish_kernel,
+        name="finish",
+        out_shape=tuple(jax.ShapeDtypeStruct(v.shape, v.dtype) for v in values),
+        in_specs=[in_vmem] * len(values),
+        out_specs=(in_vmem,) * len(values),
+    )(*values)
+
+
 def body(embeddings, row_accum, relations, relation_accum, request_rows, head_slots, tail_slots, relation_ids, own_negatives, far_negatives):
     rounds, shards, sides, slot = request_rows.shape
     inputs = dict(
@@ -545,7 +594,7 @@
         own_neg=own_negatives,
         far_neg=far_negatives,
     )
-    emb, accum, step, rel_accum = run(inputs, shards // 2, lax.axis_size("dom") // INNER, slot)
+    emb, accum, step, rel_accum = finish(*run(inputs, shards // 2, lax.axis_size("dom") // INNER, slot))
     return (emb, accum[0], step, rel_accum[0])
 
 

time: 141 us -> 130 us (0.922)
  local copies, waits for them, and re-layouts: 5.19 us -> 0 us
  Pallas kernels: 134 us -> 129 us
    pallas_call x1, Pallas kernels: 134 us -> 127 us  [run(): pl.pallas_call(functools.partial(main_kernel, zs, xs, slot, width, names)...]
    unnamed x4 -> x0, local copies, waits for them, and re-layouts: 5.19 us -> none
    pallas_call x0 -> x1, Pallas kernels: none -> 1.58 us  [finish(): pl.pallas_call(finish_kernel, name='finish', out_shape=tuple((jax.ShapeDt...]
where the time goes in v5:
time: 130 us
  Pallas kernels  129 us (99%)
    pallas_call x1, Pallas kernels, run(): pl.pallas_call(functools.partial(main_kernel, zs, xs, slot, width, names)...  127 us

profile of v5, /device:TPU:6, one launch (start us, length us, event | category | flops | bytes accessed | tf_op | source)
XLA Modules:
  0.0 129.7 jit_solution(8637593065920059641)
XLA Ops:
  0.6 127.5 %train_step.1 = (f32[64,400]{1,0:T(8,128)}, f32[1,64]{1,0:T(1,128)}, f32[5,400]{1,0:T(8,128)}, f32[1,5]{1,0:T(1,128)}) custom-call(f32[64,400]{1,0:T(8,128)} %refs_0_.1, f32[1,64]{1,0:T(1,128)} %bitcast.10, bf16[400,2560]{1,0:T(8,128)(2,1)} %bitcast.8, f32[1,5]{1,0:T(1,128)} %bitcast.11, s32[2,32,32]{2,1,0:T(8,128)} %bitcast.9, s32[2,128]{1,0:T(2,128)} %refs_5_.1, ...), custom_call_target="tpu_custom_call" | custom-call | tf_op jit(solution)/shard_map/train_step/pallas_call | solution.py:555
  128.1 1.6 %finish.1 = (f32[64,400]{1,0:T(8,128)}, f32[1,64]{1,0:T(1,128)}, f32[5,400]{1,0:T(8,128)}, f32[1,5]{1,0:T(1,128)}) custom-call(f32[64,400]{1,0:T(8,128)} %get-tuple-element.12.refs_0_, f32[1,64]{1,0:T(1,128)} %get-tuple-element.13.refs_1_, f32[5,400]{1,0:T(8,128)} %get-tuple-element.14.refs_2_, f32[1,5]{1,0:T(1,128)} %get-tuple-element.15.refs_3_), custom_call_target="tpu_custom_call" | custom-call | tf_op jit(solution)/shard_map/finish/pallas_call | solution.py:574

commit v6 on v5

--- a/solution.py
+++ b/solution.py
@@ -97,12 +97,7 @@
         self.count = hops(place.zs)
         self.far = place.zs // 2
         self.jump = place.zs // 4 + 1
-        near, rest = list(range(1, self.jump)), list(range(self.jump, self.far + 1))
-        self.order = []
-        while near or rest:
-            for lane in (near, rest):
-                if lane:
-                    self.order.append(lane.pop(0))
+        self.order = sorted(range(1, self.far + 1), key=lambda t: 1.0 * t if t < self.jump else t - self.jump + 1.1)
 
     def copy(self, src, dst, direction, t, c, hop):
         return remote(
@@ -169,8 +164,10 @@
         for direction, c in ring.each(t):
             step(direction, t, c).start()
     select(0)
-    beside()
-    for t in ring.order:
+    for number, t in enumerate(ring.order):
+        if number in beside:
+            beside[number]()
+
         for direction, c in ring.each(t):
             step(direction, t, c).wait_recv()
             if t + 1 <= ring.count[c][direction] and t + 1 != ring.jump:
@@ -218,8 +215,7 @@
             term[d, c * PER : (c + 1) * PER] = value[:, c * 128 : (c + 1) * 128]
         term[d, FULL:] = jnp.concatenate([fold(value[:, TAIL:]), jnp.zeros((8, 128), F32)], axis=0)
 
-    order = ring.order[::-1]
-    order = sorted(order, key=lambda t: (ring.far - t) if t >= ring.jump else (ring.jump - 1 - t) + 1.5)
+    order = sorted(range(1, ring.far + 1), key=lambda t: (ring.far - t) if t >= ring.jump else (ring.jump - 1 - t) + 1.5)
     for t in order:
         for d in (t,) if t == ring.far else (t, zs - t):
             for copy in exchange(d):
@@ -228,19 +224,31 @@
         copy.start()
     aside[0]()
     made = set()
+
+    def chained(t, direction, c):
+        return t < ring.count[c][direction] and t + 1 != ring.jump
+
+    def pass_on(t, direction, c):
+        d = t if direction == 0 else zs - t
+        if d not in made:
+            make_term(d)
+            made.add(d)
+        low, high = CUTS[c]
+        value = term[d, low:high]
+        if chained(t, direction, c):
+            step(direction, t + 1, c).wait_recv()
+            value = value + came[direction, t, low:high].astype(F32)
+        sent[direction, t - 1, low:high] = value.astype(BF)
+        step(direction, t, c).start()
+
+    for t in order:
+        for direction, c in ring.each(t):
+            if not chained(t, direction, c):
+                pass_on(t, direction, c)
     for number, t in enumerate(order):
         for direction, c in ring.each(t):
-            d = t if direction == 0 else zs - t
-            if d not in made:
-                make_term(d)
-                made.add(d)
-            low, high = CUTS[c]
-            value = term[d, low:high]
-            if t < ring.count[c][direction] and t + 1 != ring.jump:
-                step(direction, t + 1, c).wait_recv()
-                value = value + came[direction, t, low:high].astype(F32)
-            sent[direction, t - 1, low:high] = value.astype(BF)
-            step(direction, t, c).start()
+            if chained(t, direction, c):
+                pass_on(t, direction, c)
         if number + 1 in aside:
             aside[number + 1]()
     make_term(0)
@@ -310,13 +318,16 @@
     def rel_column(r):
         return column(n["rel_ids"][r : r + 1, :], edges)
 
-    for r in range(2):
+    def prepare(r):
         for side, name in enumerate(("own_neg", "far_neg")):
             n["count"][2 * r + side : 2 * r + side + 1, :] = counts(n[name][r : r + 1, :])
-    table_copy.wait()
-    for r in range(2):
+        if r == 0:
+            table_copy.wait()
         hot = (iota((edges, nrel), 1) == rel_column(r)).astype(BF)
         rel_vec[r, :, :width] = mm(hot, n["rel_table"][...], 1, 1)
+
+    prepare(0)
+    prepare(1)
     pl.semaphore_wait(barrier, len(everyone))
 
     def edge_step(r):
@@ -471,7 +482,7 @@
         fetch(
             place, r, slot, n["block"].at[r], n["line"].at[r], n["picked"].at[r], n["own"].at[r], n["far"].at[r], n["idx"].at[r],
             Ring(place, n["f_send"].at[r], n["f_recv"].at[r]), n["fp_send"].at[r], n["fp_recv"].at[r], n["f_self"].at[r],
-            functools.partial(rows_sum, 0) if r else (lambda: None),
+            {0: functools.partial(rows_sum, 0)} if r else {},
         )
         edge_step(r)
         steps = {0: [functools.partial(rows_start, r)]}

time: 130 us -> 128 us (0.985)
    pallas_call x1, Pallas kernels: 127 us -> 126 us  [run(): pl.pallas_call(functools.partial(main_kernel, zs, xs, slot, width, names)...]
where the time goes in v6:
time: 128 us
  Pallas kernels  128 us (100%)
    pallas_call x1, Pallas kernels, run(): pl.pallas_call(functools.partial(main_kernel, zs, xs, slot, width, names)...  126 us

profile of v6, /device:TPU:6, one launch (start us, length us, event | category | flops | bytes accessed | tf_op | source)
XLA Modules:
  0.0 128.3 jit_solution(8592762926556519632)
XLA Ops:
  0.6 126.1 %train_step.1 = (f32[64,400]{1,0:T(8,128)}, f32[1,64]{1,0:T(1,128)}, f32[5,400]{1,0:T(8,128)}, f32[1,5]{1,0:T(1,128)}) custom-call(f32[64,400]{1,0:T(8,128)} %refs_0_.1, f32[1,64]{1,0:T(1,128)} %bitcast.10, bf16[400,2560]{1,0:T(8,128)(2,1)} %bitcast.8, f32[1,5]{1,0:T(1,128)} %bitcast.11, s32[2,32,32]{2,1,0:T(8,128)} %bitcast.9, s32[2,128]{1,0:T(2,128)} %refs_5_.1, ...), custom_call_target="tpu_custom_call" | custom-call | tf_op jit(solution)/shard_map/train_step/pallas_call | solution.py:566
  126.7 1.6 %finish.1 = (f32[64,400]{1,0:T(8,128)}, f32[1,64]{1,0:T(1,128)}, f32[5,400]{1,0:T(8,128)}, f32[1,5]{1,0:T(1,128)}) custom-call(f32[64,400]{1,0:T(8,128)} %get-tuple-element.12.refs_0_, f32[1,64]{1,0:T(1,128)} %get-tuple-element.13.refs_1_, f32[5,400]{1,0:T(8,128)} %get-tuple-element.14.refs_2_, f32[1,5]{1,0:T(1,128)} %get-tuple-element.15.refs_3_), custom_call_target="tpu_custom_call" | custom-call | tf_op jit(solution)/shard_map/finish/pallas_call | solution.py:585
